TPU v7x, 32 devices: a whole 2x2x4 slice. The times are simulated.
32 devices in a mesh: ctx: 8 (over z, y), tp: 4 (over x, core).
Axes of the slice: x: 2, y: 2, z: 4, core: 2. Of those that a mesh axis runs over, the one named last changes fastest.
Arguments:
- tokens: bfloat16 [1024, 8192], P('ctx', 'tp'), may hold values from -6 to 6
- query_mr: bfloat16 [1024, 8192], P('ctx', 'tp'), may hold values from -6 to 6
- key_mr: bfloat16 [1024, 8192], P('ctx', 'tp'), may hold values from -6 to 6
- gain_mr: float32 [8192], P('tp'), may hold values from 0.5 to 1.5
- filter_mr: bfloat16 [512, 128], P('tp'), may hold values from -0.5 to 0.5
- query_li: bfloat16 [1024, 8192], P('ctx', 'tp'), may hold values from -6 to 6
- key_li: bfloat16 [1024, 8192], P('ctx', 'tp'), may hold values from -6 to 6
- gain_li: float32 [8192], P('tp'), may hold values from 0.5 to 1.5
- log_rates: float32 [16, 8192], P(None, 'tp'), may hold values from -12 to -3, as said below
- retain: float32 [1024], P('ctx'), may hold values from 0.6 to 1, as said below
- residues: float32 [16, 8192], P(None, 'tp'), may hold values from -1.5 to 1.5
- cotangent: bfloat16 [1024, 8192], P('ctx', 'tp'), may hold values from -6 to 6
Outputs:
- mixed: bfloat16 [1024, 8192], P('ctx', 'tp')
- grad_tokens: bfloat16 [1024, 8192], P('ctx', 'tp')
- grad_query_mr: bfloat16 [1024, 8192], P('ctx', 'tp')
- gradient_key_medium: bfloat16 [1024, 8192], P('ctx', 'tp')
- grad_query_li: bfloat16 [1024, 8192], P('ctx', 'tp')
- grad_key_li: bfloat16 [1024, 8192], P('ctx', 'tp')
- grad_gain_mr: float32 [8192], P('tp')
- grad_gain_li: float32 [8192], P('tp')
- grad_filter_mr: float32 [512, 128], P('tp')
- grad_residues: float32 [16, 8192], P(None, 'tp')
- grad_log_rates: float32 [16, 8192], P(None, 'tp')
Inputs may be any that keep to these rules, and one draw needn't show every extreme that they name: `log_rates`: each entry is the logarithm of a decay rate per position. `retain`: a share of state kept at a position, 1 at most positions.
All inputs are finite; a program needn't handle non-finite values.
Results may differ from a plain program's by a relative error of at most 0.0054.
Values may be sent and summed in bfloat16 or wider, within the bound.
A program may use at most 128 MiB of HBM per device.

v0:
```python
import math

import jax
import jax.numpy as jnp
from jax import lax
from jax.sharding import PartitionSpec as P

EPSILON = 1e-06
SUB_ROWS = 64
MODE_TILE = 8


def shifted(value, axis, steps):
    count = lax.axis_size(axis)
    leading, last = (max(0, -steps), min(count, count - steps))
    return lax.ppermute(value, axis, [(source, source + steps) for source in range(leading, last)])


def prefix(part, axis, combine, identity, reverse):
    count = lax.axis_size(axis)
    place = lax.axis_index(axis)
    ahead = count - 1 - place if reverse else place
    gathered = jax.tree.map(lambda a: lax.all_gather(a, axis), part)
    state = jax.tree.map(lambda a, e: jnp.zeros_like(a) + jnp.asarray(e, a.dtype), part, identity)

    def one(hop, state):
        source = count - 1 - hop if reverse else hop
        return combine(
            state, jax.tree.map(lambda a: lax.dynamic_index_in_dim(a, source, 0, False), gathered)
        )

    return lax.fori_loop(0, ahead, one, state)


def lag_tables(width):
    row_ids = lax.broadcasted_iota(jnp.int32, (width, width), 0)
    column_indices = lax.broadcasted_iota(jnp.int32, (width, width), 1)
    return (row_ids, column_indices, (row_ids - column_indices) % width)


def band_pair(filters):
    row_ids, column_indices, lag_index = lag_tables(filters.shape[1])
    table = jnp.take(filters, lag_index, axis=1)
    blank = jnp.zeros_like(table)
    return (
        jnp.where(row_ids >= column_indices, table, blank),
        jnp.where(row_ids < column_indices, table, blank),
    )


def mode_states(log_pole, retain_seq, inputs):
    count_of_rows, channels = inputs.shape
    sub = min(SUB_ROWS, count_of_rows)
    pieces = count_of_rows // sub
    log_keep = jnp.log(retain_seq).reshape(pieces, sub)
    shaped = inputs.reshape(pieces, sub, channels)
    counter = lax.broadcasted_iota(jnp.float32, (sub, 1, 1), 0) + 1.0
    triangle = (
        lax.broadcasted_iota(jnp.int32, (sub, sub), 0)
        >= lax.broadcasted_iota(jnp.int32, (sub, sub), 1)
    ).astype(jnp.float32)

    def advance(carry, piece):
        values, logs = piece
        growth_factor = counter * log_pole[None] + jnp.cumsum(logs)[:, None, None]
        scaled = values[:, None, :] * jnp.exp(-growth_factor)
        summed = jnp.einsum("tu,unc->tnc", triangle, scaled, precision=lax.Precision.HIGHEST)
        states = jnp.exp(growth_factor) * (carry[None] + summed)
        return (states[-1], states)

    start = jnp.zeros(log_pole.shape, jnp.float32)
    final, states = lax.scan(advance, start, (shaped, log_keep))
    return states.reshape(count_of_rows, log_pole.shape[0], channels)


def chain_pair(earlier, later):
    return (earlier[0] * later[0], later[0] * earlier[1] + later[1])


def body(
    tokens,
    query_mr,
    key_mr,
    gain_mr,
    filter_mr,
    query_li,
    key_li,
    gain_li,
    log_rates,
    retain,
    residues,
    cotangent,
):
    count_of_rows, channels = tokens.shape
    groups, width = filter_mr.shape
    members = channels // groups
    modes = log_rates.shape[0]
    tile = min(MODE_TILE, modes)
    full_width = channels * lax.axis_size("tp")
    factor = 1.0 / math.sqrt(count_of_rows * lax.axis_size("ctx"))
    block_count = count_of_rows // width
    x_value = tokens.astype(jnp.float32)
    query_one = query_mr.astype(jnp.float32)
    key_one = key_mr.astype(jnp.float32)
    query_two = query_li.astype(jnp.float32)
    key_two = key_li.astype(jnp.float32)
    power_in = lax.psum(jnp.sum(x_value * x_value, axis=1), "tp")
    scale_in = lax.rsqrt(power_in / full_width + EPSILON)[:, None]
    normed_in = x_value * gain_mr[None, :] * scale_in
    mixed_in = (key_one * normed_in).astype(jnp.bfloat16)
    before = shifted(mixed_in[count_of_rows - (width - 1) :], "ctx", 1)
    padded = jnp.concatenate([jnp.zeros((1, channels), jnp.bfloat16), before, mixed_in], axis=0)
    blocks = padded.reshape(block_count + 1, width, groups, members)
    beneath_diagonal_strip, upper_band = band_pair(filter_mr)
    conv_mr = jnp.einsum(
        "gij,bjgc->bigc", beneath_diagonal_strip, blocks[1:], preferred_element_type=jnp.float32
    )
    conv_mr = conv_mr + jnp.einsum(
        "gij,bjgc->bigc", upper_band, blocks[:-1], preferred_element_type=jnp.float32
    )
    conv_mr = conv_mr.reshape(count_of_rows, channels)
    middle = (x_value + query_one * conv_mr).astype(jnp.bfloat16)
    mid_value = middle.astype(jnp.float32)
    power_mid = lax.psum(jnp.sum(mid_value * mid_value, axis=1), "tp")
    scale_mid = lax.rsqrt(power_mid / full_width + EPSILON)[:, None]
    normed_mid = mid_value * gain_li[None, :] * scale_mid
    mixed_mid = key_two * normed_mid
    rates = jnp.exp(log_rates)
    log_pole = -rates
    poles = jnp.exp(log_pole)
    spread = jnp.sqrt(-jnp.expm1(-2.0 * rates))
    weight = residues * spread
    log_keep = jnp.log(retain)
    keep_total = jnp.sum(log_keep)
    cumulative_decay_product = jnp.cumsum(log_keep)[:, None, None]
    positions = lax.broadcasted_iota(jnp.float32, (count_of_rows, 1, 1), 0)
    local_states = []
    finals = []
    conv_li = jnp.zeros((count_of_rows, channels), jnp.float32)
    for start_mode in range(0, modes, tile):
        states = mode_states(log_pole[start_mode : start_mode + tile], retain, mixed_mid)
        local_states.append(states)
        finals.append(states[-1])
        conv_li = conv_li + jnp.einsum("tnc,nc->tc", states, weight[start_mode : start_mode + tile])
    decay_all = jnp.exp(count_of_rows * log_pole + keep_total)
    final_all = jnp.concatenate(finals, axis=0)
    moved = prefix(
        (decay_all, final_all),
        "ctx",
        chain_pair,
        (jnp.ones_like(decay_all), jnp.zeros_like(final_all)),
        False,
    )
    entering = moved[1]
    for start_mode in range(0, modes, tile):
        carried = jnp.exp(
            (positions + 1.0) * log_pole[None, start_mode : start_mode + tile]
            + cumulative_decay_product
        )
        conv_li = conv_li + jnp.einsum(
            "tnc,nc->tc", carried, (weight * entering)[start_mode : start_mode + tile]
        )
    mixed = (mid_value + query_two * conv_li).astype(jnp.bfloat16)
    upstream = cotangent.astype(jnp.float32)
    grad_query_li = (upstream * conv_li).astype(jnp.bfloat16)
    grad_conv_li = upstream * query_two
    retain_next = jnp.concatenate([retain[1:], jnp.ones((1,), jnp.float32)])[::-1]
    reversed_input = grad_conv_li[::-1]
    units = []
    leads = []
    for start_mode in range(0, modes, tile):
        unit = mode_states(log_pole[start_mode : start_mode + tile], retain_next, reversed_input)[
            ::-1
        ]
        units.append(unit)
        leads.append((weight * poles)[start_mode : start_mode + tile] * retain[0] * unit[0])
    lead_all = jnp.concatenate(leads, axis=0)
    moved_back = prefix(
        (decay_all, lead_all),
        "ctx",
        chain_pair,
        (jnp.ones_like(decay_all), jnp.zeros_like(lead_all)),
        True,
    )
    incoming = moved_back[1]
    adjoint_blended_inner = jnp.zeros((count_of_rows, channels), jnp.float32)
    weight_sums = []
    pole_sums = []
    for number, start_mode in enumerate(range(0, modes, tile)):
        part_pole = log_pole[None, start_mode : start_mode + tile]
        through = jnp.exp(
            (count_of_rows - 1.0 - positions) * part_pole + (keep_total - cumulative_decay_product)
        )
        adjoint = (
            weight[None, start_mode : start_mode + tile] * units[number]
            + through * incoming[None, start_mode : start_mode + tile]
        )
        carried = jnp.exp((positions + 1.0) * part_pole + cumulative_decay_product)
        states = local_states[number] + carried * entering[None, start_mode : start_mode + tile]
        earlier_states = jnp.concatenate(
            [entering[None, start_mode : start_mode + tile], states[:-1]], axis=0
        )
        adjoint_blended_inner = adjoint_blended_inner + jnp.sum(adjoint, axis=1)
        weight_sums.append(jnp.einsum("tc,tnc->nc", grad_conv_li, states))
        pole_sums.append(jnp.sum(retain[:, None, None] * adjoint * earlier_states, axis=0))
    weight_grad = jnp.concatenate(weight_sums, axis=0)
    pole_grad = jnp.concatenate(pole_sums, axis=0)
    residue_part = spread * weight_grad
    rate_part = rates * (
        residues * jnp.exp(-2.0 * rates) / spread * weight_grad - poles * pole_grad
    )
    grad_key_li = (adjoint_blended_inner * normed_mid).astype(jnp.bfloat16)
    grad_normed_mid = adjoint_blended_inner * key_two
    gain_li_part = jnp.sum(grad_normed_mid * mid_value * scale_mid, axis=0)
    inner_mid = lax.psum(jnp.sum(grad_normed_mid * gain_li[None, :] * mid_value, axis=1), "tp")
    grad_mid = (
        upstream
        + gain_li[None, :] * scale_mid * grad_normed_mid
        - mid_value * scale_mid**3 * inner_mid[:, None] / full_width
    )
    grad_query_mr = (grad_mid * conv_mr).astype(jnp.bfloat16)
    grad_conv_mr = grad_mid * query_one
    lower_wide = beneath_diagonal_strip.astype(jnp.float32)
    upper_wide = upper_band.astype(jnp.float32)
    received = shifted(grad_conv_mr[: width - 1], "ctx", -1)
    grad_padded = jnp.concatenate(
        [grad_conv_mr, received, jnp.zeros((1, channels), jnp.float32)], axis=0
    )
    grad_blocks = grad_padded.reshape(block_count + 1, width, groups, members)
    grad_mixed_in = jnp.einsum(
        "gij,bigc->bjgc", lower_wide, grad_blocks[:-1], precision=lax.Precision.HIGHEST
    )
    grad_mixed_in = grad_mixed_in + jnp.einsum(
        "gij,bigc->bjgc", upper_wide, grad_blocks[1:], precision=lax.Precision.HIGHEST
    )
    grad_mixed_in = grad_mixed_in.reshape(count_of_rows, channels)
    own_blocks = grad_conv_mr.reshape(block_count, width, groups, members)
    input_wide = blocks.astype(jnp.float32)
    table_low = jnp.einsum(
        "bigc,bjgc->gij", own_blocks, input_wide[1:], precision=lax.Precision.HIGHEST
    )
    table_up = jnp.einsum(
        "bigc,bjgc->gij", own_blocks, input_wide[:-1], precision=lax.Precision.HIGHEST
    )
    row_ids, column_indices, lag_index = lag_tables(width)
    combined = jnp.where(row_ids >= column_indices, table_low, table_up)
    filter_part = (
        jnp.zeros((groups, width), jnp.float32)
        .at[:, lag_index.reshape(-1)]
        .add(combined.reshape(groups, width * width))
    )
    gradient_key_medium = (grad_mixed_in * normed_in).astype(jnp.bfloat16)
    grad_normed_in = grad_mixed_in * key_one
    gain_mr_part = jnp.sum(grad_normed_in * x_value * scale_in, axis=0)
    inner_in = lax.psum(jnp.sum(grad_normed_in * gain_mr[None, :] * x_value, axis=1), "tp")
    grad_tokens = (
        grad_mid
        + gain_mr[None, :] * scale_in * grad_normed_in
        - x_value * scale_in**3 * inner_in[:, None] / full_width
    )
    totals = lax.psum((gain_mr_part, gain_li_part, filter_part, residue_part, rate_part), "ctx")
    return (
        mixed,
        grad_tokens.astype(jnp.bfloat16),
        grad_query_mr,
        gradient_key_medium,
        grad_query_li,
        grad_key_li,
        totals[0] * factor,
        totals[1] * factor,
        totals[2] * factor,
        totals[3] * factor,
        totals[4] * factor,
    )


def solution(mesh):
    return jax.shard_map(
        body,
        mesh=mesh,
        in_specs=(
            P("ctx", "tp"),
            P("ctx", "tp"),
            P("ctx", "tp"),
            P("tp"),
            P("tp", None),
            P("ctx", "tp"),
            P("ctx", "tp"),
            P("tp"),
            P(None, "tp"),
            P("ctx"),
            P(None, "tp"),
            P("ctx", "tp"),
        ),
        out_specs=(
            P("ctx", "tp"),
            P("ctx", "tp"),
            P("ctx", "tp"),
            P("ctx", "tp"),
            P("ctx", "tp"),
            P("ctx", "tp"),
            P("tp"),
            P("tp"),
            P("tp", None),
            P(None, "tp"),
            P(None, "tp"),
        ),
        check_vma=False,
    )
```

profile of v0, /device:TPU:0, one launch (start us, length us, event | category | flops | bytes accessed | tf_op | source)
XLA Modules:
  0.0 643.4 jit_solution(9822249258685219884)
XLA Ops:
  12.3 8.4 %psum.63 = f32[128]{0:T(128)S(1)} all-reduce(f32[128]{0:T(128)S(1)} %fusion.102), channel_id=1, replica_groups=mesh['ctx'=8,'tp'=4] {'tp'}, use_global_device_ids=true, to_apply=%region_1.0 | all-reduce | flops 128 | bytes 1024 | tf_op jit(solution)/shard_map/psum | solution.py:107
  23.6 3.5 collective-permute-start
  29.8 4.3 broadcast.240.clone2.2
  34.1 26.3 %while.82 = (s32[]{:T(128)}, f32[8,2048]{1,0:T(8,128)S(1)}, f32[2,64,8,2048]{3,2,1,0:T(8,128)}, f32[8,2048]{1,0:T(8,128)S(1)}, f32[2,64]{1,0:T(2,128)S(1)}, /*in...) while((s32[]{:T(128)}, f32[8,2048]{1,0:T(8,128)S(1)}, ...), condition=%wide.region_16.17_spmd.clone, body=%wide.region_14.16_spmd.clone.sunk | while | flops 813707264 | bytes 81660848 | solution.py:72
  34.5 6.6 %bitcast_multiply_fusion.14 = f32[64,8,2048]{2,0,1:T(8,128)S(1)} fusion(f32[64,2048]{1,0:T(8,128)S(1)} %dynamic-slice_bitcast_fusion.10, f32[8,2048]{1,0:T(8,128)S(1)} %get-tuple-element.878, f32[64]{0:T(128)S(1)} %reduce.23, f32[8,2048]{1,0:T(8,128)S(1)} %get-tuple-element.889, f32[64]{0:T(128)S(1)} %add_bitcast_fusion.10), kind=kOutput, calls=%fused_computation.53.clone.1 | convolution fusion | flops 813703168 | bytes 4850176 | tf_op jit(solution)/shard_map/while/body/eval_jaxpr/tu,unc->tnc/dot_general | solution.py:67
  44.0 3.2 copy-done.6
  47.6 6.6 %bitcast_multiply_fusion.14 = f32[64,8,2048]{2,0,1:T(8,128)S(1)} fusion(f32[64,2048]{1,0:T(8,128)S(1)} %dynamic-slice_bitcast_fusion.10, f32[8,2048]{1,0:T(8,128)S(1)} %get-tuple-element.878, f32[64]{0:T(128)S(1)} %reduce.23, f32[8,2048]{1,0:T(8,128)S(1)} %get-tuple-element.889, f32[64]{0:T(128)S(1)} %add_bitcast_fusion.10), kind=kOutput, calls=%fused_computation.53.clone.1 | convolution fusion | flops 813703168 | bytes 4850176 | tf_op jit(solution)/shard_map/while/body/eval_jaxpr/tu,unc->tnc/dot_general | solution.py:67
  60.4 4.2 broadcast.240.clone2.3
  64.7 26.5 %while.83 = (s32[]{:T(128)}, f32[8,2048]{1,0:T(8,128)S(1)}, f32[2,64,8,2048]{3,2,1,0:T(8,128)}, f32[8,2048]{1,0:T(8,128)S(1)}, f32[2,64]{1,0:T(2,128)S(1)}, /*in...) while((s32[]{:T(128)}, f32[8,2048]{1,0:T(8,128)S(1)}, ...), condition=%wide.region_19.20_spmd.clone, body=%wide.region_17.19_spmd.clone.sunk | while | flops 813707264 | bytes 81660848 | solution.py:72
  65.2 6.6 %bitcast_multiply_fusion.15 = f32[64,8,2048]{2,0,1:T(8,128)S(1)} fusion(f32[64,2048]{1,0:T(8,128)S(1)} %dynamic-slice_bitcast_fusion.11, f32[8,2048]{1,0:T(8,128)S(1)} %get-tuple-element.905, f32[64]{0:T(128)S(1)} %reduce.24, f32[8,2048]{1,0:T(8,128)S(1)} %get-tuple-element.916, f32[64]{0:T(128)S(1)} %add_bitcast_fusion.11), kind=kOutput, calls=%fused_computation.72.clone.1 | convolution fusion | flops 813703168 | bytes 4850176 | tf_op jit(solution)/shard_map/while/body/eval_jaxpr/tu,unc->tnc/dot_general | solution.py:67
  78.4 6.6 %bitcast_multiply_fusion.15 = f32[64,8,2048]{2,0,1:T(8,128)S(1)} fusion(f32[64,2048]{1,0:T(8,128)S(1)} %dynamic-slice_bitcast_fusion.11, f32[8,2048]{1,0:T(8,128)S(1)} %get-tuple-element.905, f32[64]{0:T(128)S(1)} %reduce.24, f32[8,2048]{1,0:T(8,128)S(1)} %get-tuple-element.916, f32[64]{0:T(128)S(1)} %add_bitcast_fusion.11), kind=kOutput, calls=%fused_computation.72.clone.1 | convolution fusion | flops 813703168 | bytes 4850176 | tf_op jit(solution)/shard_map/while/body/eval_jaxpr/tu,unc->tnc/dot_general | solution.py:67
  98.4 57.4 %gather_fusion = bf16[16384,128]{1,0:T(8,128)(2,1)} fusion(bf16[128,128]{0,1:T(8,128)(2,1)S(1)} %copy.108, s32[16384]{0:T(1024)S(1)} %fusion.128), kind=kCustom, calls=%fused_computation | custom fusion | bytes 8454144 | tf_op jit(solution)/shard_map/jit(_take)/gather | solution.py:43
  155.8 6.7 %copy.109 = bf16[128,128,128]{1,0,2:T(8,128)(2,1)} copy(bf16[128,128,128]{2,1,0:T(8,128)(2,1)} %bitcast.266) | data formatting | bytes 8388608 | tf_op jit(solution)/shard_map/jit(_take)/gather | solution.py:43
  162.5 5.5 fusion.80
  168.6 6.0 fusion.90
  176.5 6.1 psum.64
  185.0 4.3 broadcast.240.clone2.1
  189.3 32.0 %while.80 = (s32[]{:T(128)}, f32[8,2048]{1,0:T(8,128)}, f32[2,64,8,2048]{3,2,1,0:T(8,128)}, f32[8,2048]{1,0:T(8,128)S(1)}, f32[2,64]{1,0:T(2,128)}, /*index=5*/f...) while((s32[]{:T(128)}, f32[8,2048]{1,0:T(8,128)}, f32[2,64,8,2048]{3,2,1,0:T(8,128)}, ...), condition=%wide.region_6.7_spmd.clone, body=%wide.region_4.6_spmd.clone.sunk | while | flops 813707264 | bytes 81660848 | solution.py:72
  190.9 7.6 %bitcast_multiply_fusion.12 = f32[64,8,2048]{2,0,1:T(8,128)S(1)} fusion(f32[64,2048]{1,0:T(8,128)S(1)} %dynamic-slice_bitcast_fusion.8, f32[8,2048]{1,0:T(8,128)} %get-tuple-element.827, f32[64]{0:T(128)S(1)} %reduce.21, f32[8,2048]{1,0:T(8,128)S(1)} %get-tuple-element.838, f32[64]{0:T(128)} %add_bitcast_fusion.8), kind=kOutput, calls=%fused_computation.15.clone.1 | convolution fusion | flops 813703168 | bytes 4850176 | tf_op jit(solution)/shard_map/while/body/eval_jaxpr/tu,unc->tnc/dot_general | solution.py:67
  202.1 3.2 copy-done.1
  206.9 7.6 %bitcast_multiply_fusion.12 = f32[64,8,2048]{2,0,1:T(8,128)S(1)} fusion(f32[64,2048]{1,0:T(8,128)S(1)} %dynamic-slice_bitcast_fusion.8, f32[8,2048]{1,0:T(8,128)} %get-tuple-element.827, f32[64]{0:T(128)S(1)} %reduce.21, f32[8,2048]{1,0:T(8,128)S(1)} %get-tuple-element.838, f32[64]{0:T(128)} %add_bitcast_fusion.8), kind=kOutput, calls=%fused_computation.15.clone.1 | convolution fusion | flops 813703168 | bytes 4850176 | tf_op jit(solution)/shard_map/while/body/eval_jaxpr/tu,unc->tnc/dot_general | solution.py:67
  218.1 3.2 copy-done.1
  222.0 4.3 broadcast.240.clone2
  226.2 32.5 %while.81 = (s32[]{:T(128)}, f32[8,2048]{1,0:T(8,128)}, f32[2,64,8,2048]{3,2,1,0:T(8,128)}, f32[8,2048]{1,0:T(8,128)S(1)}, f32[2,64]{1,0:T(2,128)}, /*index=5*/f...) while((s32[]{:T(128)}, f32[8,2048]{1,0:T(8,128)}, f32[2,64,8,2048]{3,2,1,0:T(8,128)}, ...), condition=%wide.region_9.10_spmd.clone, body=%wide.region_7.9_spmd.clone.sunk | while | flops 813707264 | bytes 81660848 | solution.py:72
  228.2 7.6 %bitcast_multiply_fusion.13 = f32[64,8,2048]{2,0,1:T(8,128)S(1)} fusion(f32[64,2048]{1,0:T(8,128)S(1)} %dynamic-slice_bitcast_fusion.9, f32[8,2048]{1,0:T(8,128)} %get-tuple-element.800, f32[64]{0:T(128)S(1)} %reduce.22, f32[8,2048]{1,0:T(8,128)S(1)} %get-tuple-element.811, f32[64]{0:T(128)} %add_bitcast_fusion.9), kind=kOutput, calls=%fused_computation.34.clone.1 | convolution fusion | flops 813703168 | bytes 4850176 | tf_op jit(solution)/shard_map/while/body/eval_jaxpr/tu,unc->tnc/dot_general | solution.py:67
  239.4 3.2 copy-done.3
  244.2 7.6 %bitcast_multiply_fusion.13 = f32[64,8,2048]{2,0,1:T(8,128)S(1)} fusion(f32[64,2048]{1,0:T(8,128)S(1)} %dynamic-slice_bitcast_fusion.9, f32[8,2048]{1,0:T(8,128)} %get-tuple-element.800, f32[64]{0:T(128)S(1)} %reduce.22, f32[8,2048]{1,0:T(8,128)S(1)} %get-tuple-element.811, f32[64]{0:T(128)} %add_bitcast_fusion.9), kind=kOutput, calls=%fused_computation.34.clone.1 | convolution fusion | flops 813703168 | bytes 4850176 | tf_op jit(solution)/shard_map/while/body/eval_jaxpr/tu,unc->tnc/dot_general | solution.py:67
  255.4 3.2 copy-done.3
  261.1 7.5 %fusion.71 = f32[2048,128]{0,1:T(8,128)} fusion(f32[2,64,8,2048]{3,2,1,0:T(8,128)} %get-tuple-element.307, f32[2048,8]{0,1:T(8,128)} %get-tuple-element.573), kind=kLoop, calls=%fused_computation.97 | loop fusion | flops 3932160 | bytes 9502720 | tf_op jit(solution)/shard_map/tnc,nc->tc/dot_general | solution.py:144
  268.7 3.9 fusion.70
  272.7 7.4 %while.79 = (s32[]{:T(128)}, f32[16,2048]{1,0:T(8,128)S(1)}, s32[]{:T(128)}, f32[8,16,2048]{2,1,0:T(8,128)}, f32[8,16,2048]{2,1,0:T(8,128)}, /*index=5*/s32[]{:T(128)}, s32[]{:T(128)}, s32[]{:T(128)}, s32[]{:T(128)}) while((s32[]{:T(128)}, f32[16,2048]{1,0:T(8,128)S(1)}, s32[]{:T(128)}, f32[8,16,2048]{2,1,0:T(8,128)}, ...), condition=%wide.region_21.22_spmd, body=%wide.region_20.21_spmd.sunk | while | flops 65542 | bytes 524439 | solution.py:32
  280.2 32.2 %all-gather.9.cloned.1.call-done = f32[128,2048]{1,0:T(8,128)} async-done(((f32[16,2048]{1,0:T(8,128)}), f32[128,2048]{1,0:T(8,128)}) %all-gather.9.cloned.1.call-update) | async-done | bytes 1048592 | tf_op jit(solution)/shard_map/all_gather | solution.py:23
  313.8 12.7 %multiply_reduce_fusion.1 = (f32[2048,8]{0,1:T(8,128)S(1)}, f32[2048,8]{0,1:T(8,128)S(1)}, f32[128,8,2048]{2,1,0:T(8,128)S(1)}, f32[128,8,2048]{2,1,0:T(8,128)}) fusion(f32[2048,128]{0,1:T(8,128)} %get-tuple-element.542, f32[8,2048]{1,0:T(8,128)S(1)} %get-tuple-element.549, f32[128]{0:T(128)S(1)} %reduce.10, f32[8,2048]{1,0:T(8,128)S(1)} %get-tuple-element.966, ...), kind=kLoop, calls=%fused_computation.99 | loop fusion | flops 25133056 | bytes 34997248 | tf_op jit(solution)/shard_map/tc,tnc->nc/dot_general | solution.py:204
  326.5 4.2 slice.150
  330.7 8.8 %slice.149 = f32[127,8,2048]{2,1,0:T(8,128)} slice(f32[128,8,2048]{2,1,0:T(8,128)} %get-tuple-element.529), slice={[0:127], [0:8], [0:2048]} | slice | bytes 16646144 | tf_op jit(solution)/shard_map/slice | solution.py:201
  340.8 14.4 %fusion.68 = (f32[8,2048]{1,0:T(8,128)S(1)}, f32[128,2048]{1,0:T(8,128)S(1)}, f32[128,2048]{1,0:T(8,128)}, f32[8,2048]{1,0:T(8,128)S(1)}) fusion(f32[127,8,2048]{2,1,0:T(8,128)} %slice.149, f32[1,8,2048]{2,1,0:T(8,128)} %get-tuple-element.548, f32[128,8,2048]{2,1,0:T(8,128)S(1)} %bitcast.261, f32[128]{0:T(128)S(1)} %copy-done.38, ...), kind=kLoop, calls=%fused_computation.91 | loop fusion | flops 41385984 | bytes 36177408 | tf_op jit(solution)/shard_map/reduce_sum | solution.py:205
  357.8 6.4 psum.65
  364.2 8.3 %multiply_reduce_fusion.3 = (f32[2048,128]{0,1:T(8,128)S(1)}, f32[2048,128]{0,1:T(8,128)S(1)}) fusion(f32[2048,8]{0,1:T(8,128)S(1)} %copy-done.28, f32[128]{0:T(128)S(1)} %copy-done.42, f32[8,2048]{1,0:T(8,128)S(1)} %get-tuple-element.964, f32[128]{0:T(128)S(1)} %copy-done.44, f32[8,2048]{1,0:T(8,128)S(1)} %get-tuple-element.966, f32[2048,8]{0,1:T(8,128)S(1)} %copy-done.27), kind=kLoop, calls=%fused_computation.101 | loop fusion | flops 16252928 | bytes 2360320 | tf_op jit(solution)/shard_map/tnc,nc->tc/dot_general | solution.py:160
  372.6 3.7 multiply_convert_fusion
  381.8 6.7 %fusion.152 = f32[128,128,128]{2,1,0:T(8,128)S(1)} fusion(f32[128,128,16]{0,2,1:T(8,128)S(1)} %bitcast.267, bf16[128,128,16]{0,2,1:T(8,128)(2,1)S(1)} %bitcast.273), kind=kOutput, calls=%fused_computation.260 | convolution fusion | flops 402653184 | bytes 9961472 | tf_op jit(solution)/shard_map/bigc,bjgc->gij/dot_general | solution.py:239
  388.6 10.2 %broadcast_select_fusion.3 = f32[128,128,128]{2,1,0:T(8,128)} fusion(f32[128,128,128]{2,1,0:T(8,128)S(1)} %fusion.152, pred[128,128]{1,0:T(8,128)(4,1)S(1)} %copy-done.30, f32[128,128,16]{0,2,1:T(8,128)S(1)} %bitcast.268, bf16[128,128,16]{0,2,1:T(8,128)(2,1)S(1)} %bitcast.275), kind=kOutput, calls=%fused_computation.121 | convolution fusion | flops 404750336 | bytes 18366464 | tf_op jit(solution)/shard_map/bigc,bjgc->gij/dot_general | solution.py:242
  398.8 9.4 %copy.160 = f32[128,128,128]{0,2,1:T(8,128)} copy(f32[128,128,128]{2,1,0:T(8,128)} %broadcast_select_fusion.3) | data formatting | bytes 16777216 | tf_op jit(solution)/shard_map/reshape | solution.py:250
  408.1 88.2 %scatter_custom_fusion = f32[128,128]{0,1:T(8,128)} fusion(s32[16384]{0:T(1024)} %bitcast.285, f32[16384,128]{1,0:T(8,128)} %bitcast.270, f32[]{:T(128)} %constant.155.clone.1), kind=kCustom, calls=%fused_computation.230 | custom fusion | flops 2097152 | bytes 66048 | tf_op jit(solution)/shard_map/scatter-add | solution.py:250
  497.2 5.9 fusion.78
  503.1 74.9 %all-reduce.6.cloned.1.call-done = (f32[128,128]{0,1:T(8,128)}, f32[16,2048]{1,0:T(8,128)}, f32[16,2048]{1,0:T(8,128)}) async-done(((f32[128,128]{0,1:T(8,128)}, f32[16,2048]{1,0:T(8,128)}, f32[16,2048]{1,0:T(8,128)}), (f32[128,128]{0,1:T(8,128)}, f32[16,2048]{1,0:T(8,128)}, f32[16,2048]{1,0:T(8,128)})) %all-reduce.6.cloned.1.call-update) | async-done | bytes 327696 | tf_op jit(solution)/shard_map/psum | solution.py:261
  584.4 6.0 fusion.93
  593.3 35.3 %all-reduce.2 = (f32[2048]{0:T(1024)S(1)}, f32[2048]{0:T(1024)S(1)}) all-reduce(f32[2048]{0:T(1024)S(1)} %get-tuple-element.445, f32[2048]{0:T(1024)S(1)} %get-tuple-element.447), channel_id=1, replica_groups=mesh['ctx'=8,'tp'=4] {'ctx'}, use_global_device_ids=true, to_apply=%region_29.30 | all-reduce | flops 4096 | bytes 32768 | tf_op jit(solution)/shard_map/psum | solution.py:261
  629.2 5.6 psum.66
  (275 shorter events, 99.5 us)
Async XLA Ops:
  7.2 20.9 %copy-start.14 = (bf16[128,2048]{1,0:T(8,128)(2,1)S(1)}, bf16[128,2048]{1,0:T(8,128)(2,1)}, u32[]{:S(2)}) copy-start(bf16[128,2048]{1,0:T(8,128)(2,1)} %param.35) | copy-start | bytes 1572868
  7.2 20.9 %copy-start.15 = (bf16[128,2048]{1,0:T(8,128)(2,1)S(1)}, bf16[128,2048]{1,0:T(8,128)(2,1)}, u32[]{:S(2)}) copy-start(bf16[128,2048]{1,0:T(8,128)(2,1)} %param.29) | copy-start | bytes 1572868
  7.2 265.5 %all-gather.7.cloned.1.call-start = ((), (), s32[]{:S(2)}) async-start(), calls=%async_computation | async-start | bytes 1179648 | tf_op jit(solution)/shard_map/all_gather | solution.py:23
  11.1 261.7 %all-gather.11.cloned.1.call-start = ((), (), s32[]{:S(2)}) async-start(), calls=%async_computation.2 | async-start | bytes 1179648 | tf_op jit(solution)/shard_map/all_gather | solution.py:23
  21.2 6.9 %copy-start.36 = (f32[128]{0:T(128)}, f32[128]{0:T(128)S(1)}, u32[]{:S(2)}) copy-start(f32[128]{0:T(128)S(1)} %get-tuple-element.566) | copy-start | bytes 1540
  23.6 144.4 %collective-permute-start = (bf16[127,2048]{1,0:T(8,128)(2,1)}, bf16[127,2048]{1,0:T(8,128)(2,1)S(1)}, u32[]{:S(2)}, u32[]{:S(2)}) collective-permute-start(bf16[127,2048]{1,0:T(8,128)(2,1)} %slice.135), channel_id=1, source_target_pairs={{0,4},{4,8},{8,12},{12,16},{16,20},{20,24},{24,28},{1,5},{5,9},{9,... | collective-permute-start | bytes 1560584 | tf_op jit(solution)/shard_map/ppermute | solution.py:16
  64.7 26.5 %copy-start.24 = (f32[16,2048]{1,0:T(8,128)S(1)}, f32[16,2048]{1,0:T(8,128)}, u32[]{:S(2)}) copy-start(f32[16,2048]{1,0:T(8,128)} %get-tuple-element.535) | copy-start | bytes 393220
  64.7 26.5 %copy-start.38 = (f32[128]{0:T(128)S(1)}, f32[128]{0:T(128)}, u32[]{:S(2)}) copy-start(f32[128]{0:T(128)} %param.33) | copy-start | bytes 1540
  64.7 33.6 %copy-start.31 = (bf16[128,128]{1,0:T(8,128)(2,1)S(1)}, bf16[128,128]{1,0:T(8,128)(2,1)}, u32[]{:S(2)}) copy-start(bf16[128,128]{1,0:T(8,128)(2,1)} %param.28) | copy-start | bytes 98308
  93.4 219.0 %all-gather.9.cloned.1.call-start = ((), (), s32[]{:S(2)}) async-start(), calls=%async_computation.1 | async-start | bytes 1179648 | tf_op jit(solution)/shard_map/all_gather | solution.py:23
  94.1 74.5 %copy-start.32 = (pred[128,128]{1,0:T(8,128)(4,1)}, pred[128,128]{1,0:T(8,128)(4,1)S(1)}, u32[]{:S(2)}) copy-start(pred[128,128]{1,0:T(8,128)(4,1)S(1)} %iota_compare_fusion.8) | copy-start | bytes 49156
  94.2 68.4 %copy-start.29 = (pred[128,128]{1,0:T(8,128)(4,1)}, pred[128,128]{1,0:T(8,128)(4,1)S(1)}, u32[]{:S(2)}) copy-start(pred[128,128]{1,0:T(8,128)(4,1)S(1)} %get-tuple-element.576) | copy-start | bytes 49156
  94.2 74.4 %copy-start.34 = (pred[128,128]{1,0:T(8,128)(4,1)}, pred[128,128]{1,0:T(8,128)(4,1)S(1)}, u32[]{:S(2)}) copy-start(pred[128,128]{1,0:T(8,128)(4,1)S(1)} %get-tuple-element.577) | copy-start | bytes 49156
  94.6 219.1 %copy-start.41 = (f32[128]{0:T(128)}, f32[128]{0:T(128)S(1)}, u32[]{:S(2)}) copy-start(f32[128]{0:T(128)S(1)} %reduce.10) | copy-start | bytes 1540
  97.6 65.0 %copy-start.12 = (bf16[128,2048]{0,1:T(8,128)(2,1)}, bf16[128,2048]{0,1:T(8,128)(2,1)S(1)}, u32[]{:S(2)}) copy-start(bf16[128,2048]{0,1:T(8,128)(2,1)S(1)} %copy.107) | copy-start | bytes 1572868
  168.6 7.6 %copy-start.9 = (bf16[128,2048]{1,0:T(8,128)(2,1)S(1)}, bf16[128,2048]{1,0:T(8,128)(2,1)}, u32[]{:S(2)}) copy-start(bf16[128,2048]{1,0:T(8,128)(2,1)} %param.24) | copy-start | bytes 1572868
  168.6 7.6 %copy-start.17 = (bf16[128,2048]{1,0:T(8,128)(2,1)S(1)}, bf16[128,2048]{1,0:T(8,128)(2,1)}, u32[]{:S(2)}) copy-start(bf16[128,2048]{1,0:T(8,128)(2,1)} %param.25) | copy-start | bytes 1572868
  174.6 8.5 %copy-start.25 = (f32[2048]{0:T(1024)S(1)}, f32[2048]{0:T(1024)}, u32[]{:S(2)}) copy-start(f32[2048]{0:T(1024)} %param.31) | copy-start | bytes 24580
  190.9 8.4 %copy-start = (f32[2,64,8,2048]{3,2,1,0:T(8,128)S(1)}, f32[2,64,8,2048]{3,2,1,0:T(8,128)}, u32[]{:S(2)}) copy-start(f32[2,64,8,2048]{3,2,1,0:T(8,128)} %get-tuple-element.828) | copy-start | bytes 25165828 | tf_op jit(solution)/shard_map/while
  206.9 8.4 %copy-start = (f32[2,64,8,2048]{3,2,1,0:T(8,128)S(1)}, f32[2,64,8,2048]{3,2,1,0:T(8,128)}, u32[]{:S(2)}) copy-start(f32[2,64,8,2048]{3,2,1,0:T(8,128)} %get-tuple-element.828) | copy-start | bytes 25165828 | tf_op jit(solution)/shard_map/while
  228.2 8.4 %copy-start.2 = (f32[2,64,8,2048]{3,2,1,0:T(8,128)S(1)}, f32[2,64,8,2048]{3,2,1,0:T(8,128)}, u32[]{:S(2)}) copy-start(f32[2,64,8,2048]{3,2,1,0:T(8,128)} %get-tuple-element.801) | copy-start | bytes 25165828 | tf_op jit(solution)/shard_map/while
  244.2 8.4 %copy-start.2 = (f32[2,64,8,2048]{3,2,1,0:T(8,128)S(1)}, f32[2,64,8,2048]{3,2,1,0:T(8,128)}, u32[]{:S(2)}) copy-start(f32[2,64,8,2048]{3,2,1,0:T(8,128)} %get-tuple-element.801) | copy-start | bytes 25165828 | tf_op jit(solution)/shard_map/while
  261.1 7.5 %copy-start.4 = (f32[2,64,8,2048]{3,2,1,0:T(8,128)S(1)}, f32[2,64,8,2048]{3,2,1,0:T(8,128)}, u32[]{:S(2)}) copy-start(f32[2,64,8,2048]{3,2,1,0:T(8,128)} %get-tuple-element.308) | copy-start | bytes 25165828
  272.6 41.2 %copy-start.44 = (f32[128]{0:T(128)S(1)}, f32[128]{0:T(128)}, u32[]{:S(2)}) copy-start(f32[128]{0:T(128)} %iota_add_fusion) | copy-start | bytes 1540
  272.6 305.4 %all-reduce.6.cloned.1.call-start = ((), (), s32[]{:S(2)}) async-start(), calls=%async_computation.3 | async-start | bytes 655360 | tf_op jit(solution)/shard_map/psum | solution.py:261
  326.5 13.1 %slice-start.2 = ((s8[8388608]{0:T(1024)(128)(4,1)}), s8[4194304]{0:T(1024)(128)(4,1)S(1)}, s32[]{:S(2)}) async-start(s8[8388608]{0:T(1024)(128)(4,1)} %bitcast.263), calls=%async_computation.6 | async-start | bytes 8388608
  330.7 8.9 %slice-start = ((s8[8388608]{0:T(1024)(128)(4,1)}), s8[4194304]{0:T(1024)(128)(4,1)S(1)}, s32[]{:S(2)}) async-start(s8[8388608]{0:T(1024)(128)(4,1)} %bitcast.259), calls=%async_computation.4 | async-start | bytes 8388608
  330.7 8.9 %slice-start.1 = ((s8[8388608]{0:T(1024)(128)(4,1)}), s8[4194304]{0:T(1024)(128)(4,1)S(1)}, s32[]{:S(2)}) async-start(s8[8388608]{0:T(1024)(128)(4,1)} %bitcast.259), calls=%async_computation.5 | async-start | bytes 8388608
  330.7 10.0 %slice-start.3 = ((s8[8388608]{0:T(1024)(128)(4,1)}), s8[4194304]{0:T(1024)(128)(4,1)S(1)}, s32[]{:S(2)}) async-start(s8[8388608]{0:T(1024)(128)(4,1)} %bitcast.263), calls=%async_computation.7 | async-start | bytes 8388608
  330.7 10.0 %copy-start.45 = (f32[128]{0:T(128)S(1)}, f32[128]{0:T(128)}, u32[]{:S(2)}) copy-start(f32[128]{0:T(128)} %broadcast_subtract_fusion) | copy-start | bytes 1540
  330.7 10.0 %copy-start.46 = (f32[128]{0:T(128)S(1)}, f32[128]{0:T(128)}, u32[]{:S(2)}) copy-start(f32[128]{0:T(128)} %iota_subtract_fusion.1) | copy-start | bytes 1540
  340.7 14.4 %copy-start.19 = (bf16[128,2048]{1,0:T(8,128)(2,1)S(1)}, bf16[128,2048]{1,0:T(8,128)(2,1)}, u32[]{:S(2)}) copy-start(bf16[128,2048]{1,0:T(8,128)(2,1)} %param.30) | copy-start | bytes 1572868
  340.8 14.4 %copy-start.40 = (f32[128]{0:T(128)S(1)}, f32[128]{0:T(128)}, u32[]{:S(2)}) copy-start(f32[128]{0:T(128)} %copy-done.39) | copy-start | bytes 1540
  355.1 9.1 %copy-start.27 = (f32[2048,8]{0,1:T(8,128)S(1)}, f32[2048,8]{0,1:T(8,128)}, u32[]{:S(2)}) copy-start(f32[2048,8]{0,1:T(8,128)} %get-tuple-element.559) | copy-start | bytes 196612
  355.1 9.1 %copy-start.28 = (f32[2048,8]{0,1:T(8,128)S(1)}, f32[2048,8]{0,1:T(8,128)}, u32[]{:S(2)}) copy-start(f32[2048,8]{0,1:T(8,128)} %get-tuple-element.560) | copy-start | bytes 196612
  355.1 9.1 %copy-start.42 = (f32[128]{0:T(128)S(1)}, f32[128]{0:T(128)}, u32[]{:S(2)}) copy-start(f32[128]{0:T(128)} %copy-done.41) | copy-start | bytes 1540
  364.2 8.3 %copy-start.11 = (f32[128,2048]{1,0:T(8,128)S(1)}, f32[128,2048]{1,0:T(8,128)}, u32[]{:S(2)}) copy-start(f32[128,2048]{1,0:T(8,128)} %get-tuple-element.534) | copy-start | bytes 3145732
  364.2 8.3 %copy-start.47 = (f32[128]{0:T(128)S(1)}, f32[128]{0:T(128)}, u32[]{:S(2)}) copy-start(f32[128]{0:T(128)} %psum.65) | copy-start | bytes 1540
  380.0 202.7 %collective-permute-start.1 = (f32[127,2048]{1,0:T(8,128)}, f32[127,2048]{1,0:T(8,128)}, u32[]{:S(2)}, u32[]{:S(2)}) collective-permute-start(f32[127,2048]{1,0:T(8,128)} %bitcast.271), channel_id=1, source_target_pairs={{4,0},{8,4},{12,8},{16,12},{20,16},{24,20},{28,24},{5,1},{9,5},{13... | collective-permute-start | bytes 3121160 | tf_op jit(solution)/shard_map/ppermute | solution.py:16
  381.8 6.8 %copy-start.21 = (bf16[128,2048]{0,1:T(8,128)(2,1)S(1)}, bf16[128,2048]{0,1:T(8,128)(2,1)}, u32[]{:S(2)}) copy-start(bf16[128,2048]{0,1:T(8,128)(2,1)} %copy-done.20) | copy-start | bytes 1572868
  398.8 97.6 %copy-start.22 = (f32[16,2048]{1,0:T(8,128)S(1)}, f32[16,2048]{1,0:T(8,128)}, u32[]{:S(2)}) copy-start(f32[16,2048]{1,0:T(8,128)} %param.32) | copy-start | bytes 393220
  398.8 97.6 %copy-start.23 = (f32[16,2048]{1,0:T(8,128)S(1)}, f32[16,2048]{1,0:T(8,128)}, u32[]{:S(2)}) copy-start(f32[16,2048]{1,0:T(8,128)} %param.34) | copy-start | bytes 393220
  398.8 98.4 %copy-start.35 = (pred[128,128]{1,0:T(8,128)(4,1)S(1)}, pred[128,128]{1,0:T(8,128)(4,1)}, u32[]{:S(2)}) copy-start(pred[128,128]{1,0:T(8,128)(4,1)} %copy-done.34) | copy-start | bytes 49156
  503.1 81.3 %copy-start.33 = (pred[128,128]{1,0:T(8,128)(4,1)S(1)}, pred[128,128]{1,0:T(8,128)(4,1)}, u32[]{:S(2)}) copy-start(pred[128,128]{1,0:T(8,128)(4,1)} %copy-done.32) | copy-start | bytes 49156
  584.4 7.6 %copy-start.10 = (bf16[128,2048]{1,0:T(8,128)(2,1)S(1)}, bf16[128,2048]{1,0:T(8,128)(2,1)}, u32[]{:S(2)}) copy-start(bf16[128,2048]{1,0:T(8,128)(2,1)} %param.26) | copy-start | bytes 1572868
  584.4 7.6 %copy-start.26 = (f32[2048]{0:T(1024)S(1)}, f32[2048]{0:T(1024)}, u32[]{:S(2)}) copy-start(f32[2048]{0:T(1024)} %param.27) | copy-start | bytes 24580
  584.4 7.6 %copy-start.37 = (f32[128]{0:T(128)S(1)}, f32[128]{0:T(128)}, u32[]{:S(2)}) copy-start(f32[128]{0:T(128)} %copy-done.36) | copy-start | bytes 1540
  590.5 45.0 %copy-start.43 = (f32[128]{0:T(128)S(1)}, f32[128]{0:T(128)}, u32[]{:S(2)}) copy-start(f32[128]{0:T(128)} %get-tuple-element.565) | copy-start | bytes 1540
  (18 other events, 85.6 us)
Sparse Core Ops, SparseCore 0:
  11.2 44.0 all-gather.6
  93.5 39.5 all-gather.10
  272.7 39.5 all-gather.8
  497.3 80.6 all-reduce.5
where the time goes:
time: 653 us; the launch traced here: 643 us
  other arithmetic  180 us (28%)
  local copies, waits for them, and re-layouts  176 us (27%)
  waiting for transfers between devices  107 us (16%)
  matrix products  97.4 us (15%)
  blocking collectives  61.7 us (9%)
  between operations  14.6 us (2%)
    scatter-add x1, other arithmetic, body(): filter_part = jnp.zeros((groups, width), jnp.float32).at[:, lag_index.res...  88.2 us
    psum x1, waiting for transfers between devices, body(): lax.psum((gain_mr_part, gain_li_part, filter_part, residue_part, rate_par...  74.9 us
    gather x2, local copies, waits for them, and re-layouts, band_pair(): table = jnp.take(filters, lag_index, axis=1)  64.1 us
    dot_general x8, matrix products, advance(): jnp.einsum('tu,unc->tnc', triangle, scaled, precision=lax.Precision.HIGHEST)  57.1 us
    psum x1, blocking collectives, body(): lax.psum((gain_mr_part, gain_li_part, filter_part, residue_part, rate_par...  35.3 us
    all_gather x3, waiting for transfers between devices, prefix(): gathered = jax.tree.map(lambda a: lax.all_gather(a, axis), part)  32.2 us
    while x40, local copies, waits for them, and re-layouts  28.3 us
    dynamic_update_slice x8, local copies, waits for them, and re-layouts, mode_states(): final, states = lax.scan(advance, start, (shaped, log_keep))  22.6 us
  transfers between devices with their start and end apart: 6, of which 2 were waited for; matrix products, arithmetic and copies ran while one was open for 54% of the time, Pallas kernels for 0%

commit v1 on v0

v1 whole, which is shorter than its diff:
```python
import functools
import math

import jax
import jax.numpy as jnp
from jax import lax
from jax.experimental import pallas as pl
from jax.experimental.pallas import tpu as pltpu
from jax.sharding import PartitionSpec as P

EPSILON = 1e-06
LANES = 128
F32 = jnp.float32
BF16 = jnp.bfloat16
MESH = pl.DeviceIdType.MESH


def vmem(count):
    return [pl.BlockSpec(memory_space=pltpu.VMEM)] * count


def local_call(kernel, name, outs, args, scratch=(), flops=10_000_000):
    return pl.pallas_call(
        kernel,
        name=name,
        out_shape=[jax.ShapeDtypeStruct(s, d) for s, d in outs],
        in_specs=vmem(len(args)),
        out_specs=vmem(len(outs)),
        scratch_shapes=list(scratch),
        cost_estimate=pl.CostEstimate(flops=flops, bytes_accessed=8_000_000, transcendentals=0),
    )(*args)


def exchange(items, sizes, cid, name):
    count = len(items)
    axes = []
    for _, axis, _ in items:
        if axis not in axes:
            axes.append(axis)
    remote = sum(sizes[axis] - 1 for _, axis, _ in items)

    def kernel(*refs):
        ins, outs = refs[:count], refs[count : 2 * count]
        send, recv, own = refs[2 * count :]
        barrier = pltpu.get_barrier_semaphore()
        greeted = 0
        for axis in axes:
            me = lax.axis_index(axis)
            for step in range(1, sizes[axis]):
                peer = lax.rem(me + step, sizes[axis])
                pl.semaphore_signal(barrier, inc=1, device_id={axis: peer}, device_id_type=MESH)
                greeted += 1
        pl.semaphore_wait(barrier, greeted)
        copies = []
        slot = 0
        for number, (_, axis, scatter) in enumerate(items):
            me = lax.axis_index(axis)
            for step in range(1, sizes[axis]):
                peer = lax.rem(me + step, sizes[axis])
                source = ins[number].at[peer] if scatter else ins[number]
                copy = pltpu.make_async_remote_copy(
                    src_ref=source,
                    dst_ref=outs[number].at[me],
                    send_sem=send.at[slot],
                    recv_sem=recv.at[slot],
                    device_id={axis: peer},
                    device_id_type=MESH,
                )
                copy.start()
                copies.append(copy)
                slot += 1
            source = ins[number].at[me] if scatter else ins[number]
            copy = pltpu.make_async_copy(source, outs[number].at[me], own.at[number])
            copy.start()
            copies.append(copy)
        for copy in copies:
            copy.wait()

    outs = []
    for array, axis, scatter in items:
        shape = array.shape if scatter else (sizes[axis],) + array.shape
        outs.append(jax.ShapeDtypeStruct(shape, array.dtype))
    return pl.pallas_call(
        kernel,
        name=name,
        out_shape=outs,
        in_specs=vmem(count),
        out_specs=vmem(count),
        scratch_shapes=[
            pltpu.SemaphoreType.DMA((remote,)),
            pltpu.SemaphoreType.DMA((remote,)),
            pltpu.SemaphoreType.DMA((count,)),
        ],
        compiler_params=pltpu.CompilerParams(collective_id=cid, has_side_effects=True),
    )(*[array for array, _, _ in items])


def column(row):
    return jnp.broadcast_to(row, (LANES, LANES)).T


def row8(partial):
    total = jnp.sum(partial, axis=1, keepdims=True)
    return jnp.broadcast_to(total, partial.shape).T[:8]


def lane_tile(j):
    return pl.ds(pl.multiple_of(j * LANES, LANES), LANES)


def total_row(ref):
    out = ref[0]
    for k in range(1, ref.shape[0]):
        out = out + ref[k]
    return out[:1]


def begin_kernel(modes, x_ref, cot_ref, q_ref, keep_ref, p_ref, w_ref, pow_ref, r_ref, g_ref, lead_ref):
    rows, channels = x_ref.shape
    tiles = channels // LANES
    lanes = lax.broadcasted_iota(jnp.int32, (8, LANES), 1)
    run = keep_ref[...]
    step = 1
    while step < LANES:
        run = run * jnp.where(lanes >= step, pltpu.roll(run, step, 1), 1.0)
        step *= 2
    r_ref[...] = run
    r_col = column(run[:1])
    total = jnp.zeros((rows, LANES), F32)
    for j in range(tiles):
        at = slice(j * LANES, (j + 1) * LANES)
        x = x_ref[:, at].astype(F32)
        total = total + x * x
        g_ref[pl.ds(j, rows, stride=tiles), :] = (
            cot_ref[:, at].astype(F32) * q_ref[:, at].astype(F32) * r_col
        )
    pow_ref[...] = row8(total)
    sub = min(8, tiles)
    for b in range(tiles // sub):
        where = [pl.ds(n * tiles + b * sub, sub) for n in range(modes)]
        pole = [p_ref[at, :] for at in where]

        def back(i, units, b=b, pole=pole):
            t = rows - 1 - i
            g = g_ref[pl.ds(pl.multiple_of(t * tiles + b * sub, sub), sub), :]
            return tuple(pole[n] * units[n] + g for n in range(modes))

        units = lax.fori_loop(
            0, rows, back, tuple(jnp.zeros((sub, LANES), F32) for _ in range(modes)), unroll=4
        )
        for n in range(modes):
            lead_ref[where[n], :] = (w_ref[where[n], :] * pole[n] * units[n]).astype(BF16)


def carried(part_ref, r_all_ref, pass_ref, ahead, reverse):
    count = part_ref.shape[0]
    order = range(count - 1, 0, -1) if reverse else range(count - 1)
    acc = jnp.zeros(pass_ref.shape, F32)
    for m in order:
        share = jnp.broadcast_to(r_all_ref[m][:1, LANES - 1 :], (1, LANES))
        new = part_ref[m].astype(F32) + pass_ref[...] * share * acc
        live = m > ahead if reverse else m < ahead
        acc = jnp.where(live, new, acc)
    return acc


def adjoint_kernel(
    modes, g_ref, p_ref, w_ref, pass_ref, lead_ref, r_all_ref, r_ref, v_ref, q_out_ref, v3_ref
):
    rows, channels = v_ref.shape
    tiles = channels // LANES
    r_row = r_ref[:1, :]
    r_end = jnp.broadcast_to(r_row[:, LANES - 1 :], (1, LANES))
    q_out_ref[...] = carried(lead_ref, r_all_ref, pass_ref, lax.axis_index("ctx"), True) * r_end
    sub = min(8, tiles)
    for b in range(tiles // sub):
        where = [pl.ds(n * tiles + b * sub, sub) for n in range(modes)]
        pole = [p_ref[at, :] for at in where]
        weight = [w_ref[at, :] for at in where]
        last = pl.ds((rows - 1) * tiles + b * sub, sub)
        g = g_ref[last, :]
        start = [q_out_ref[where[n], :] + weight[n] * g for n in range(modes)]
        v3_ref[last, :] = functools.reduce(lambda a, c: a + c, start)

        def back(i, adj, b=b, pole=pole, weight=weight):
            at = pl.ds(pl.multiple_of((rows - 2 - i) * tiles + b * sub, sub), sub)
            g = g_ref[at, :]
            adj = tuple(pole[n] * adj[n] + weight[n] * g for n in range(modes))
            sums = list(adj)
            while len(sums) > 1:
                sums = [sums[k] + sums[k + 1] for k in range(0, len(sums), 2)]
            v3_ref[at, :] = sums[0]
            return adj

        lax.fori_loop(0, rows - 1, back, tuple(start), unroll=2)
    inverse = 1.0 / column(r_row)
    for j in range(tiles):
        v_ref[:, j * LANES : (j + 1) * LANES] = v3_ref[pl.ds(j, rows, stride=tiles), :] * inverse


def mix_kernel(width, x_ref, key_ref, gain_ref, pow_ref, mixed_ref):
    scale = column(lax.rsqrt(total_row(pow_ref) / width + EPSILON))
    for j in range(x_ref.shape[1] // LANES):
        at = slice(j * LANES, (j + 1) * LANES)
        normed = x_ref[:, at].astype(F32) * gain_ref[:, at] * scale
        mixed_ref[:, at] = (key_ref[:, at].astype(F32) * normed).astype(BF16)


def conv_kernel(
    members, x_ref, q_ref, mixed_ref, prev_ref, flip_ref, v_ref, key_ref, gain_ref,
    conv_ref, mid_ref, sums_ref,
):
    rows, channels = x_ref.shape
    fold = LANES // members
    row_ids = lax.broadcasted_iota(jnp.int32, (rows, LANES), 0)
    col_ids = lax.broadcasted_iota(jnp.int32, (rows, LANES), 1)
    owner = col_ids // members
    fresh = lax.axis_index("ctx") > 0

    def tile(j, sums):
        at = lane_tile(j)
        prev = prev_ref[:, at]
        prev = jnp.where(fresh, prev, jnp.zeros_like(prev))
        both = jnp.concatenate([prev, mixed_ref[:, at]], axis=0)
        taps = flip_ref[pl.ds(pl.multiple_of(j * fold, fold), fold), :]
        conv = jnp.zeros((rows, LANES), F32)
        for g in range(fold):
            table = pltpu.roll(
                jnp.broadcast_to(taps[g : g + 1], (rows, LANES)), 0, 1, stride=1, stride_axis=0
            )
            low = jnp.where(row_ids >= col_ids, table, 0.0).astype(BF16)
            high = jnp.where(row_ids < col_ids, table, 0.0).astype(BF16)
            out = jnp.dot(
                jnp.concatenate([high, low], axis=1), both, preferred_element_type=F32
            )
            conv = jnp.where(owner == g, out, conv)
        conv_ref[:, at] = conv
        mid = (x_ref[:, at].astype(F32) + q_ref[:, at].astype(F32) * conv).astype(BF16)
        mid_ref[:, at] = mid
        mid = mid.astype(F32)
        inner = v_ref[:, at] * key_ref[:, at].astype(F32) * gain_ref[:, at] * mid
        return (sums[0] + mid * mid, sums[1] + inner)

    zero = jnp.zeros((rows, LANES), F32)
    power, inner = lax.fori_loop(0, channels // LANES, tile, (zero, zero))
    sums_ref[0] = row8(power)
    sums_ref[1] = row8(inner)


def middle_kernel(
    width, mid_ref, key_ref, gain_ref, v_ref, cot_ref, qmr_ref, conv_ref, r_ref, sums_ref,
    gkey_ref, gmid_ref, gq_ref, gconv_ref, gain_part_ref, u_ref,
):
    rows, channels = v_ref.shape
    tiles = channels // LANES
    sums = sums_ref[0]
    for k in range(1, sums_ref.shape[0]):
        sums = sums + sums_ref[k]
    scale = column(lax.rsqrt(sums[0][:1] / width + EPSILON))
    pull = scale * scale * scale * column(sums[1][:1]) / width
    inverse = 1.0 / column(r_ref[:1, :])
    for j in range(tiles):
        at = slice(j * LANES, (j + 1) * LANES)
        mid = mid_ref[:, at].astype(F32)
        key = key_ref[:, at].astype(F32)
        gain = gain_ref[:, at]
        v = v_ref[:, at]
        normed = mid * gain * scale
        gkey_ref[:, at] = (v * normed).astype(BF16)
        u_ref[pl.ds(j, rows, stride=tiles), :] = key * normed * inverse
        grad = v * key
        gain_part_ref[:, at] = jnp.sum(grad * mid * scale, axis=0, keepdims=True)
        gmid = cot_ref[:, at].astype(F32) + gain * scale * grad - mid * pull
        gmid_ref[:, at] = gmid
        gq_ref[:, at] = (gmid * conv_ref[:, at]).astype(BF16)
        gconv_ref[:, at] = (gmid * qmr_ref[:, at].astype(F32)).astype(BF16)


def finish_kernel(modes, u_ref, p_ref, r_ref, out_ref):
    tiles = p_ref.shape[0] // modes
    rows = u_ref.shape[0] // tiles
    r_end = jnp.broadcast_to(r_ref[:1, LANES - 1 :], (1, LANES))
    sub = min(8, tiles)
    for b in range(tiles // sub):
        where = [pl.ds(n * tiles + b * sub, sub) for n in range(modes)]
        pole = [p_ref[at, :] for at in where]

        def step(t, states, b=b, pole=pole):
            u = u_ref[pl.ds(pl.multiple_of(t * tiles + b * sub, sub), sub), :]
            return tuple(pole[n] * states[n] + u for n in range(modes))

        states = lax.fori_loop(
            0, rows, step, tuple(jnp.zeros((sub, LANES), F32) for _ in range(modes)), unroll=4
        )
        for n in range(modes):
            out_ref[where[n], :] = (states[n] * r_end).astype(BF16)


def state_kernel(
    modes, u_ref, g_ref, p_ref, w_ref, pass_ref, fin_ref, r_all_ref, r_ref, q_ref, c_ref,
    mid_ref, cot_ref, qli_ref, mixed_ref, gq_ref, res_ref, rate_ref, y_ref, in_ref,
):
    rows, channels = mid_ref.shape
    tiles = channels // LANES
    in_ref[...] = carried(fin_ref, r_all_ref, pass_ref, lax.axis_index("ctx"), False)
    sub = min(8, tiles)
    half = min(8, modes)
    zero = jnp.zeros((sub, LANES), F32)
    for b in range(tiles // sub):
        for first in range(0, modes, half):
            where = [pl.ds((first + n) * tiles + b * sub, sub) for n in range(half)]
            pole = [p_ref[at, :] for at in where]
            weight = [w_ref[at, :] for at in where]

            def step(t, carry, b=b, first=first, pole=pole, weight=weight):
                at = pl.ds(pl.multiple_of(t * tiles + b * sub, sub), sub)
                u = u_ref[at, :]
                g = g_ref[at, :]
                states, slopes, wsum, psum = carry
                slopes = tuple(pole[n] * slopes[n] + states[n] for n in range(half))
                states = tuple(pole[n] * states[n] + u for n in range(half))
                wsum = tuple(wsum[n] + g * states[n] for n in range(half))
                psum = tuple(psum[n] + g * slopes[n] for n in range(half))
                sums = [weight[n] * states[n] for n in range(half)]
                while len(sums) > 1:
                    sums = [sums[k] + sums[k + 1] for k in range(0, len(sums), 2)]
                if first == 0:
                    y_ref[at, :] = sums[0]
                else:
                    y_ref[at, :] = y_ref[at, :] + sums[0]
                return (states, slopes, wsum, psum)

            begin = tuple(in_ref[at, :] for at in where)
            zeros = (zero,) * half
            _, slopes, wsum, psum = lax.fori_loop(
                0, rows, step, (begin, zeros, zeros, zeros), unroll=2
            )
            for n in range(half):
                at = where[n]
                pgrad = weight[n] * psum[n] + q_ref[at, :] * slopes[n]
                res_ref[at, :] = c_ref[0, at, :] * wsum[n]
                rate_ref[at, :] = c_ref[1, at, :] * wsum[n] - c_ref[2, at, :] * pgrad
    r_col = column(r_ref[:1, :])
    for j in range(tiles):
        at = slice(j * LANES, (j + 1) * LANES)
        conv = y_ref[pl.ds(j, rows, stride=tiles), :] * r_col
        mixed_ref[:, at] = (
            mid_ref[:, at].astype(F32) + qli_ref[:, at].astype(F32) * conv
        ).astype(BF16)
        gq_ref[:, at] = (cot_ref[:, at].astype(F32) * conv).astype(BF16)


def back_kernel(
    members, width, gconv_ref, next_ref, mixed_ref, prev_ref, filt_ref, x_ref, key_ref, gain_ref,
    pow_ref, gkey_ref, gnorm_ref, gain_part_ref, inner_ref, fgrad_ref,
):
    rows, channels = x_ref.shape
    fold = LANES // members
    row_ids = lax.broadcasted_iota(jnp.int32, (rows, LANES), 0)
    col_ids = lax.broadcasted_iota(jnp.int32, (rows, LANES), 1)
    owner = col_ids // members
    flip = jnp.where(row_ids + col_ids == rows - 1, 1.0, 0.0).astype(BF16)
    place = lax.axis_index("ctx")
    fresh = place > 0
    more = place < lax.axis_size("ctx") - 1
    scale = column(lax.rsqrt(total_row(pow_ref) / width + EPSILON))

    def tile(j, inner):
        at = lane_tile(j)
        prev = prev_ref[:, at]
        prev = jnp.where(fresh, prev, jnp.zeros_like(prev))
        later = next_ref[:, at]
        later = jnp.where(more, later, jnp.zeros_like(later))
        own = gconv_ref[:, at]
        both = jnp.concatenate([own, later], axis=0)
        turned = jnp.concatenate(
            [
                jnp.dot(flip, mixed_ref[:, at], preferred_element_type=F32).astype(BF16),
                jnp.dot(flip, prev, preferred_element_type=F32).astype(BF16),
            ],
            axis=0,
        )
        rows_at = pl.ds(pl.multiple_of(j * fold, fold), fold)
        taps = filt_ref[rows_at, :]
        gmix = jnp.zeros((rows, LANES), F32)
        grads = []
        for g in range(fold):
            table = pltpu.roll(
                jnp.broadcast_to(taps[g : g + 1], (rows, LANES)), 0, 1, stride=1, stride_axis=0
            )
            low = jnp.where(col_ids >= row_ids, table, 0.0).astype(BF16)
            high = jnp.where(col_ids < row_ids, table, 0.0).astype(BF16)
            out = jnp.dot(jnp.concatenate([low, high], axis=1), both, preferred_element_type=F32)
            gmix = jnp.where(owner == g, out, gmix)
            mine = jnp.where(owner == g, own, jnp.zeros_like(own))
            pair = lax.dot_general(
                turned, mine, (((1,), (1,)), ((), ())), preferred_element_type=F32
            )
            pair = jnp.where(col_ids >= rows - 1 - row_ids, pair[:rows], pair[rows:])
            pair = pltpu.roll(pair, 1, 1, stride=1, stride_axis=0)
            grads.append(jnp.sum(pair, axis=0, keepdims=True))
        fgrad_ref[rows_at, :] = jnp.concatenate(grads, axis=0)
        x = x_ref[:, at].astype(F32)
        gain = gain_ref[:, at]
        gkey_ref[:, at] = (gmix * (x * gain * scale)).astype(BF16)
        gnorm = gmix * key_ref[:, at].astype(F32)
        gnorm_ref[:, at] = gnorm
        gain_part_ref[:, at] = jnp.sum(gnorm * x * scale, axis=0, keepdims=True)
        return inner + gnorm * gain * x

    inner = lax.fori_loop(0, channels // LANES, tile, jnp.zeros((rows, LANES), F32))
    inner_ref[...] = row8(inner)


def last_kernel(
    width, factor, x_ref, gain_ref, gmid_ref, gnorm_ref, pow_ref, inner_ref, parts_ref,
    out_ref, sum_ref,
):
    scale = column(lax.rsqrt(total_row(pow_ref) / width + EPSILON))
    pull = scale * scale * scale * column(total_row(inner_ref)) / width
    for j in range(x_ref.shape[1] // LANES):
        at = slice(j * LANES, (j + 1) * LANES)
        out_ref[:, at] = (
            gmid_ref[:, at]
            + gain_ref[:, at] * scale * gnorm_ref[:, at]
            - x_ref[:, at].astype(F32) * pull
        ).astype(BF16)
    total = parts_ref[0].astype(F32)
    for k in range(1, parts_ref.shape[0]):
        total = total + parts_ref[k].astype(F32)
    sum_ref[...] = (total * factor).astype(BF16)


def body(
    sizes,
    tokens,
    query_mr,
    key_mr,
    gain_mr,
    filter_mr,
    query_li,
    key_li,
    gain_li,
    log_rates,
    retain,
    residues,
    cotangent,
):
    rows, channels = tokens.shape
    groups, taps = filter_mr.shape
    members = channels // groups
    modes = log_rates.shape[0]
    tiles = channels // LANES
    ctx, tp = sizes["ctx"], sizes["tp"]
    width = channels * tp
    factor = 1.0 / math.sqrt(rows * ctx)
    flat = (modes * tiles, LANES)
    full = (rows, channels)

    rates = jnp.exp(log_rates.reshape(flat))
    resid = residues.reshape(flat)
    poles = jnp.exp(-rates)
    spread = jnp.sqrt(-jnp.expm1(-2.0 * rates))
    weight = resid * spread
    passing = jnp.exp(-rows * rates)
    consts = jnp.stack([spread, rates * resid * jnp.exp(-2.0 * rates) / spread, rates * poles])
    keep = jnp.broadcast_to(retain[None, :], (8, rows))
    wide = filter_mr.astype(F32)
    flipped = jnp.concatenate([wide[:, :1], wide[:, :0:-1]], axis=1)
    gain_mr = gain_mr[None, :]
    gain_li = gain_li[None, :]

    power, shares, g_seq, lead = local_call(
        functools.partial(begin_kernel, modes),
        "begin",
        [((8, rows), F32), ((8, rows), F32), ((rows * tiles, LANES), F32), (flat, BF16)],
        (tokens, cotangent, query_li, keep, poles, weight),
    )
    power_all, = exchange([(power, "tp", False)], sizes, 1, "gather_power")
    mixed_in, = local_call(
        functools.partial(mix_kernel, width), "mix", [(full, BF16)],
        (tokens, key_mr, gain_mr, power_all),
    )
    before = lax.ppermute(mixed_in, "ctx", [(k, k + 1) for k in range(ctx - 1)])
    lead_all, shares_all = exchange(
        [(lead, "ctx", False), (shares, "ctx", False)], sizes, 2, "gather_lead"
    )
    v, pulled = local_call(
        functools.partial(adjoint_kernel, modes),
        "adjoint",
        [(full, F32), (flat, F32)],
        (g_seq, poles, weight, passing, lead_all, shares_all, shares),
        [pltpu.VMEM((rows * tiles, LANES), F32)],
    )
    conv, middle, sums = local_call(
        functools.partial(conv_kernel, members),
        "conv",
        [(full, F32), (full, BF16), ((2, 8, rows), F32)],
        (tokens, query_mr, mixed_in, before, flipped, v, key_li, gain_li),
    )
    sums_all, = exchange([(sums, "tp", False)], sizes, 3, "gather_middle")
    grad_key_li, grad_mid, grad_query_mr, grad_conv, gain_li_part, u_seq = local_call(
        functools.partial(middle_kernel, width),
        "middle",
        [
            (full, BF16), (full, F32), (full, BF16), (full, BF16), ((1, channels), F32),
            ((rows * tiles, LANES), F32),
        ],
        (middle, key_li, gain_li, v, cotangent, query_mr, conv, shares, sums_all),
    )
    after = lax.ppermute(grad_conv, "ctx", [(k + 1, k) for k in range(ctx - 1)])
    final, = local_call(
        functools.partial(finish_kernel, modes), "finish", [(flat, BF16)], (u_seq, poles, shares)
    )
    final_all, = exchange([(final, "ctx", False)], sizes, 4, "gather_state")
    mixed, grad_query_li, residue_part, rate_part = local_call(
        functools.partial(state_kernel, modes),
        "state",
        [(full, BF16), (full, BF16), (flat, F32), (flat, F32)],
        (
            u_seq, g_seq, poles, weight, passing, final_all, shares_all, shares, pulled, consts,
            middle, cotangent, query_li,
        ),
        [pltpu.VMEM((rows * tiles, LANES), F32), pltpu.VMEM(flat, F32)],
    )
    gradient_key_medium, grad_norm, gain_mr_part, inner, filter_part = local_call(
        functools.partial(back_kernel, members, width),
        "back",
        [(full, BF16), (full, F32), ((1, channels), F32), ((8, rows), F32), ((groups, taps), F32)],
        (grad_conv, after, mixed_in, before, wide, tokens, key_mr, gain_mr, power_all),
    )
    parts = jnp.concatenate(
        [
            residue_part, rate_part, filter_part,
            gain_mr_part.reshape(tiles, LANES), gain_li_part.reshape(tiles, LANES),
        ],
        axis=0,
    ).astype(BF16)
    height = parts.shape[0]
    piece = -(-height // (16 * ctx)) * 16
    parts = jnp.pad(parts, ((0, piece * ctx - height), (0, 0))).reshape(ctx, piece, LANES)
    inner_all, parts_all = exchange(
        [(inner, "tp", False), (parts, "ctx", True)], sizes, 5, "gather_last"
    )
    grad_tokens, sums_own = local_call(
        functools.partial(last_kernel, width, factor),
        "last",
        [(full, BF16), ((piece, LANES), BF16)],
        (tokens, gain_mr, grad_mid, grad_norm, power_all, inner_all, parts_all),
    )
    totals, = exchange([(sums_own, "ctx", False)], sizes, 6, "gather_totals")
    totals = totals.reshape(ctx * piece, LANES)[:height].astype(F32)
    size = modes * tiles
    return (
        mixed,
        grad_tokens,
        grad_query_mr,
        gradient_key_medium,
        grad_query_li,
        grad_key_li,
        totals[2 * size + groups : 2 * size + groups + tiles].reshape(channels),
        totals[2 * size + groups + tiles :].reshape(channels),
        totals[2 * size : 2 * size + groups],
        totals[:size].reshape(modes, channels),
        totals[size : 2 * size].reshape(modes, channels),
    )


def solution(mesh):
    return jax.shard_map(
        functools.partial(body, dict(mesh.shape)),
        mesh=mesh,
        in_specs=(
            P("ctx", "tp"),
            P("ctx", "tp"),
            P("ctx", "tp"),
            P("tp"),
            P("tp", None),
            P("ctx", "tp"),
            P("ctx", "tp"),
            P("tp"),
            P(None, "tp"),
            P("ctx"),
            P(None, "tp"),
            P("ctx", "tp"),
        ),
        out_specs=(
            P("ctx", "tp"),
            P("ctx", "tp"),
            P("ctx", "tp"),
            P("ctx", "tp"),
            P("ctx", "tp"),
            P("ctx", "tp"),
            P("tp"),
            P("tp"),
            P("tp", None),
            P(None, "tp"),
            P(None, "tp"),
        ),
        check_vma=False,
    )
```

time: 653 us -> 156 us (0.24); the launches traced: 643 us -> 155 us
  other arithmetic: 180 us -> 5.94 us
  local copies, waits for them, and re-layouts: 176 us -> 8.74 us
  Pallas kernels: 0 us -> 132 us
  waiting for transfers between devices: 107 us -> 1.97 us
  matrix products: 97.4 us -> 0 us
  blocking collectives: 61.7 us -> 0 us
  between operations: 14.6 us -> 0.83 us
    pallas_call x0 -> x15, Pallas kernels: none -> 132 us  [the longest x6 74 us: exchange(): pl.pallas_call(kernel, name=name, out_shape=outs, in_specs=vmem(count), o...]
    dot_general x14 -> x0, matrix products: 97.4 us -> none  [the longest x8 57.1 us: advance(): jnp.einsum('tu,unc->tnc', triangle, scaled, precision=lax.Precision.HIGHEST)]
    scatter-add x1 -> x0, other arithmetic: 88.2 us -> none  [body(): filter_part = jnp.zeros((groups, width), jnp.float32).at[:, lag_index.res...]
    psum x1 -> x0, waiting for transfers between devices: 74.9 us -> none  [body(): lax.psum((gain_mr_part, gain_li_part, filter_part, residue_part, rate_par...]
    gather x2 -> x0, local copies, waits for them, and re-layouts: 64.1 us -> none  [band_pair(): table = jnp.take(filters, lag_index, axis=1)]
    psum x5 -> x0, blocking collectives: 61.7 us -> none  [the longest x1 35.3 us: body(): lax.psum((gain_mr_part, gain_li_part, filter_part, residue_part, rate_par...]
    dot_general x4 -> x0, other arithmetic: 32.5 us -> none  [the longest x1 12.7 us: body(): weight_sums.append(jnp.einsum('tc,tnc->nc', grad_conv_li, states))]
    all_gather x3 -> x0, waiting for transfers between devices: 32.2 us -> none  [prefix(): gathered = jax.tree.map(lambda a: lax.all_gather(a, axis), part)]
  transfers between devices with their start and end apart: 6 -> 2, of which waited for: 2 -> 1; matrix products, arithmetic and copies ran while one was open for 54% -> 3% of each run, Pallas kernels for 0% -> 24%
where the time goes in v1:
time: 156 us; the launch traced here: 155 us
  Pallas kernels  132 us (85%)
  local copies, waits for them, and re-layouts  8.74 us (6%)
  other arithmetic  5.94 us (4%)
  starting transfers between devices  5.4 us (3%)
  waiting for transfers between devices  1.97 us (1%)
    pallas_call x6, Pallas kernels, exchange(): pl.pallas_call(kernel, name=name, out_shape=outs, in_specs=vmem(count), o...  74 us
    pallas_call x9, Pallas kernels, local_call(): pl.pallas_call(kernel, name=name, out_shape=[jax.ShapeDtypeStruct(s, d) f...  58.5 us
    ppermute x1, starting transfers between devices, body(): before = lax.ppermute(mixed_in, 'ctx', [(k, k + 1) for k in range(ctx - 1)])  4.11 us
  transfers between devices with their start and end apart: 2, of which 1 were waited for; matrix products, arithmetic and copies ran while one was open for 3% of the time, Pallas kernels for 24%

profile of v1, /device:TPU:0, one launch (start us, length us, event | category | flops | bytes accessed | tf_op | source)
XLA Modules:
  0.0 155.4 jit_solution(2820270546370132167)
XLA Ops:
  0.6 1.1 fusion.2
  1.7 0.7 exp.46.p_ref
  2.4 0.7 reshape.139.w_ref
  3.1 0.0 copy-done.7
  3.1 0.6 broadcast_in_dim.13.keep_ref
  3.7 4.6 %begin.1 = (f32[8,128]{1,0:T(8,128)}, f32[8,128]{1,0:T(8,128)}, f32[2048,128]{1,0:T(8,128)}, bf16[256,128]{1,0:T(8,128)(2,1)}) custom-call(bf16[128,2048]{1,0:T(8,128)(2,1)} %x_ref.9, bf16[128,2048]{1,0:T(8,128)(2,1)} %cot_ref.5, bf16[128,2048]{1,0:T(8,128)(2,1)} %qli_ref.1, f32[8,128]{1,0:T(8,128)} %broadcast_in_dim.13.keep_ref, f32[256,128]{1,0:T(8,128)} %exp.46.p_ref, ...), custom_call_target="tpu_custom_call" | custom-call | flops 10000000 | bytes 8000000 | tf_op jit(solution)/shard_map/begin/pallas_call | solution.py:23
  8.3 5.9 %gather_power.1.pow_ref = f32[4,8,128]{2,1,0:T(8,128)} custom-call(f32[8,128]{1,0:T(8,128)} %get-tuple-element.41.refs_0_), custom_call_target="tpu_custom_call" | custom-call | tf_op jit(solution)/shard_map/gather_power/pallas_call | solution.py:83
  14.3 0.0 copy-start.1
  14.3 2.3 %mix.1.mixed_ref = bf16[128,2048]{1,0:T(8,128)(2,1)} custom-call(bf16[128,2048]{1,0:T(8,128)(2,1)} %x_ref.9, bf16[128,2048]{1,0:T(8,128)(2,1)} %key_ref.7, f32[1,2048]{1,0:T(1,128)} %bitcast.15, f32[4,8,128]{2,1,0:T(8,128)} %gather_power.1.pow_ref), custom_call_target="tpu_custom_call" | custom-call | flops 10000000 | bytes 8000000 | tf_op jit(solution)/shard_map/mix/pallas_call | solution.py:23
  16.5 4.1 %collective-permute-start = (bf16[128,2048]{1,0:T(8,128)(2,1)}, bf16[128,2048]{1,0:T(8,128)(2,1)S(1)}, u32[]{:S(2)}, u32[]{:S(2)}) collective-permute-start(bf16[128,2048]{1,0:T(8,128)(2,1)} %mix.1.mixed_ref), channel_id=1, source_target_pairs={{0,4},{4,8},{8,12},{12,16},{16,20},{20,24},{24,28},{1,5},{5,9},{9,... | collective-permute-start | bytes 1572872 | tf_op jit(solution)/shard_map/ppermute | solution.py:484
  20.7 0.0 copy-done.1
  20.7 0.1 slice.34
  20.8 0.0 copy-done.4
  20.8 0.6 convert_element_type.12.filt_ref
  21.4 0.7 exp.48.pass_ref
  22.1 0.1 rev.3
  22.2 19.3 %gather_lead.1 = (bf16[8,256,128]{2,1,0:T(8,128)(2,1)}, f32[8,8,128]{2,1,0:T(8,128)}) custom-call(bf16[256,128]{1,0:T(8,128)(2,1)} %get-tuple-element.43.refs_0_, f32[8,128]{1,0:T(8,128)} %get-tuple-element.44.refs_1_.r_ref), custom_call_target="tpu_custom_call" | custom-call | tf_op jit(solution)/shard_map/gather_lead/pallas_call | solution.py:83
  41.6 6.3 %adjoint.1 = (f32[128,2048]{1,0:T(8,128)}, f32[256,128]{1,0:T(8,128)}) custom-call(f32[2048,128]{1,0:T(8,128)} %get-tuple-element.42.g_ref, f32[256,128]{1,0:T(8,128)} %exp.46.p_ref, f32[256,128]{1,0:T(8,128)} %reshape.139.w_ref, f32[256,128]{1,0:T(8,128)} %exp.48.pass_ref, bf16[8,256,128]{2,1,0:T(8,128)(2,1)} %get-tuple-element.45.lead_ref, ...), custom_call_target="tpu_custom_call" | custom-call | flops 10000000 | bytes 8000000 | tf_op jit(solution)/shard_map/adjoint/pallas_call | solution.py:23
  47.9 0.7 pad_maximum_fusion.1.flip_ref
  48.6 0.1 fusion
  48.7 0.8 pad_maximum_fusion.c_ref
  49.5 0.0 collective-permute-done.prev_ref
  49.5 0.8 copy-done
  50.4 8.9 %conv.1 = (f32[128,2048]{1,0:T(8,128)}, bf16[128,2048]{1,0:T(8,128)(2,1)}, f32[2,8,128]{2,1,0:T(8,128)}) custom-call(bf16[128,2048]{1,0:T(8,128)(2,1)} %x_ref.9, bf16[128,2048]{1,0:T(8,128)(2,1)} %qmr_ref.1, bf16[128,2048]{1,0:T(8,128)(2,1)} %mix.1.mixed_ref, bf16[128,2048]{1,0:T(8,128)(2,1)} %copy-done, f32[128,128]{1,0:T(8,128)} %pad_maximum_fusion.1.flip_ref, ...), custom_call_target="tpu_custom_call" | custom-call | flops 10000000 | bytes 8000000 | tf_op jit(solution)/shard_map/conv/pallas_call | solution.py:23
  59.3 5.0 %gather_middle.1.sums_ref = f32[4,2,8,128]{3,2,1,0:T(8,128)} custom-call(f32[2,8,128]{2,1,0:T(8,128)} %get-tuple-element.50.refs_0_), custom_call_target="tpu_custom_call" | custom-call | tf_op jit(solution)/shard_map/gather_middle/pallas_call | solution.py:83
  64.3 5.3 %middle.1 = (bf16[128,2048]{1,0:T(8,128)(2,1)}, f32[128,2048]{1,0:T(8,128)}, bf16[128,2048]{1,0:T(8,128)(2,1)}, bf16[128,2048]{1,0:T(8,128)(2,1)}, f32[1,2048]{1,0:T(1,128)}, /*index=5*/f32[2048,128]{1,0:T(8,128)}) custom-call(bf16[128,2048]{1,0:T(8,128)(2,1)} %get-tuple-element.48.mid_ref, bf16[128,2048]{1,0:T(8,128)(2,1)} %key_ref.6, f32[1,2048]{1,0:T(1,128)} %bitcast.19, ...), custom_call_target="tpu_custom_call" | custom-call | flops 10000000 | bytes 8000000 | tf_op jit(solution)/shard_map/middle/pallas_call | solution.py:23
  69.6 3.3 %finish.1.refs_0_ = bf16[256,128]{1,0:T(8,128)(2,1)} custom-call(f32[2048,128]{1,0:T(8,128)} %get-tuple-element.51.u_ref, f32[256,128]{1,0:T(8,128)} %exp.46.p_ref, f32[8,128]{1,0:T(8,128)} %get-tuple-element.44.refs_1_.r_ref), custom_call_target="tpu_custom_call" | custom-call | flops 10000000 | bytes 8000000 | tf_op jit(solution)/shard_map/finish/pallas_call | solution.py:23
  73.0 21.6 %gather_state.1.fin_ref = bf16[8,256,128]{2,1,0:T(8,128)(2,1)} custom-call(bf16[256,128]{1,0:T(8,128)(2,1)} %finish.1.refs_0_), custom_call_target="tpu_custom_call" | custom-call | tf_op jit(solution)/shard_map/gather_state/pallas_call | solution.py:83
  94.6 0.0 copy-done.2
  94.6 1.3 collective-permute-start.1
  95.9 0.0 copy-start.6
  95.9 11.7 %state.1 = (bf16[128,2048]{1,0:T(8,128)(2,1)}, bf16[128,2048]{1,0:T(8,128)(2,1)}, f32[256,128]{1,0:T(8,128)}, f32[256,128]{1,0:T(8,128)}) custom-call(f32[2048,128]{1,0:T(8,128)} %get-tuple-element.51.u_ref, f32[2048,128]{1,0:T(8,128)} %get-tuple-element.42.g_ref, f32[256,128]{1,0:T(8,128)} %exp.46.p_ref, f32[256,128]{1,0:T(8,128)} %reshape.139.w_ref, ...), custom_call_target="tpu_custom_call" | custom-call | flops 10000000 | bytes 8000000 | tf_op jit(solution)/shard_map/state/pallas_call | solution.py:23
  107.6 0.9 convert_dynamic-update-slice_fusion.1
  108.6 2.0 %collective-permute-done.1.next_ref = bf16[128,2048]{1,0:T(8,128)(2,1)S(1)} collective-permute-done((bf16[128,2048]{1,0:T(8,128)(2,1)S(1)}, bf16[128,2048]{1,0:T(8,128)(2,1)S(1)}, u32[]{:S(2)}, u32[]{:S(2)}) %collective-permute-start.1) | collective-permute-done | bytes 524320 | tf_op jit(solution)/shard_map/ppermute | solution.py:511
  110.6 0.8 copy-done.3
  111.4 13.0 %back.1 = (bf16[128,2048]{1,0:T(8,128)(2,1)}, f32[128,2048]{1,0:T(8,128)}, f32[1,2048]{1,0:T(1,128)}, f32[8,128]{1,0:T(8,128)}, f32[128,128]{1,0:T(8,128)}) custom-call(bf16[128,2048]{1,0:T(8,128)(2,1)} %get-tuple-element.55.gconv_ref, bf16[128,2048]{1,0:T(8,128)(2,1)} %copy-done.3, bf16[128,2048]{1,0:T(8,128)(2,1)} %mix.1.mixed_ref, ...), custom_call_target="tpu_custom_call" | custom-call | flops 10000000 | bytes 8000000 | tf_op jit(solution)/shard_map/back/pallas_call | solution.py:23
  124.4 0.7 convert_reduce_fusion.1
  125.1 0.9 convert_dynamic-update-slice_fusion.2
  126.0 0.7 pad.4
  126.7 11.9 %gather_last.1 = (f32[4,8,128]{2,1,0:T(8,128)}, bf16[8,96,128]{2,1,0:T(8,128)(2,1)}) custom-call(f32[8,128]{1,0:T(8,128)} %get-tuple-element.57.refs_0_, bf16[8,96,128]{2,1,0:T(8,128)(2,1)} %bitcast.14), custom_call_target="tpu_custom_call" | custom-call | tf_op jit(solution)/shard_map/gather_last/pallas_call | solution.py:83
  138.6 2.9 %last.1 = (bf16[128,2048]{1,0:T(8,128)(2,1)}, bf16[96,128]{1,0:T(8,128)(2,1)}) custom-call(bf16[128,2048]{1,0:T(8,128)(2,1)} %x_ref.9, f32[1,2048]{1,0:T(1,128)} %bitcast.17, f32[128,2048]{1,0:T(8,128)} %get-tuple-element.54.gmid_ref, f32[128,2048]{1,0:T(8,128)} %get-tuple-element.56.gnorm_ref, f32[4,8,128]{2,1,0:T(8,128)} %gather_power.1.pow_ref, ...), custom_call_target="tpu_custom_call" | custom-call | flops 10000000 | bytes 8000000 | tf_op jit(solution)/shard_map/last/pallas_call | solution.py:23
  141.5 10.3 %gather_totals.1 = bf16[8,96,128]{2,1,0:T(8,128)(2,1)} custom-call(bf16[96,128]{1,0:T(8,128)(2,1)} %get-tuple-element.70.refs_0_), custom_call_target="tpu_custom_call" | custom-call | tf_op jit(solution)/shard_map/gather_totals/pallas_call | solution.py:83
  151.8 0.0 slice-start
  151.8 0.9 slice-done
  152.8 0.6 slice.37
  153.4 0.6 slice_bitcast_fusion
  154.0 0.7 reshape.135
  154.7 0.7 reshape.136
  (17 shorter events, 0.2 us)
Async XLA Ops:
  2.4 0.7 copy-start.7
  14.3 6.4 %copy-start.1 = (bf16[128,128]{1,0:T(8,128)(2,1)S(1)}, bf16[128,128]{1,0:T(8,128)(2,1)}, u32[]{:S(2)}) copy-start(bf16[128,128]{1,0:T(8,128)(2,1)} %param.16) | copy-start | bytes 98308
  16.5 4.2 %copy-start.4 = (f32[16,2048]{1,0:T(8,128)S(1)}, f32[16,2048]{1,0:T(8,128)}, u32[]{:S(2)}) copy-start(f32[16,2048]{1,0:T(8,128)} %param.22) | copy-start | bytes 393220
  16.5 33.0 %collective-permute-start = (bf16[128,2048]{1,0:T(8,128)(2,1)}, bf16[128,2048]{1,0:T(8,128)(2,1)S(1)}, u32[]{:S(2)}, u32[]{:S(2)}) collective-permute-start(bf16[128,2048]{1,0:T(8,128)(2,1)} %mix.1.mixed_ref), channel_id=1, source_target_pairs={{0,4},{4,8},{8,12},{12,16},{16,20},{20,24},{24,28},{1,5},{5,9},{9,... | collective-permute-start | bytes 1572872 | tf_op jit(solution)/shard_map/ppermute | solution.py:484
  49.5 0.8 copy-start
  73.0 21.6 %copy-start.2 = (bf16[128,2048]{1,0:T(8,128)(2,1)S(1)}, bf16[128,2048]{1,0:T(8,128)(2,1)}, u32[]{:S(2)}) copy-start(bf16[128,2048]{1,0:T(8,128)(2,1)} %get-tuple-element.55.gconv_ref) | copy-start | bytes 1572868
  94.6 16.0 %collective-permute-start.1 = (bf16[128,2048]{1,0:T(8,128)(2,1)S(1)}, bf16[128,2048]{1,0:T(8,128)(2,1)S(1)}, u32[]{:S(2)}, u32[]{:S(2)}) collective-permute-start(bf16[128,2048]{1,0:T(8,128)(2,1)S(1)} %copy-done.2), channel_id=1, source_target_pairs={{4,0},{8,4},{12,8},{16,12},{20,16},{24,20},{28,24},{5,1},{9,5},{13... | collective-permute-start | bytes 1572872 | tf_op jit(solution)/shard_map/ppermute | solution.py:511
  95.9 11.7 %copy-start.6 = (f32[1,2048]{1,0:T(1,128)S(1)}, f32[1,2048]{1,0:T(1,128)}, u32[]{:S(2)}) copy-start(f32[1,2048]{1,0:T(1,128)} %get-tuple-element.62) | copy-start | bytes 24580
  107.6 1.0 copy-start.5
  110.6 0.8 copy-start.3
  151.8 0.9 slice-start

commit v2 on v1

--- a/solution.py
+++ b/solution.py
@@ -95,6 +95,94 @@
     )(*[array for array, _, _ in items])
 
 
+class Link:
+    def __init__(self, sizes, send, recv):
+        self.sizes, self.send, self.recv, self.used = sizes, send, recv, 0
+
+    def greet(self, axes):
+        barrier = pltpu.get_barrier_semaphore()
+        greeted = 0
+        for axis in axes:
+            me = lax.axis_index(axis)
+            for step in range(1, self.sizes[axis]):
+                peer = lax.rem(me + step, self.sizes[axis])
+                pl.semaphore_signal(barrier, inc=1, device_id={axis: peer}, device_id_type=MESH)
+                greeted += 1
+        pl.semaphore_wait(barrier, greeted)
+
+    def copy(self, source, target, axis, peer):
+        slot = self.used
+        self.used += 1
+        return pltpu.make_async_remote_copy(
+            src_ref=source,
+            dst_ref=target,
+            send_sem=self.send.at[slot],
+            recv_sem=self.recv.at[slot],
+            device_id={axis: peer},
+            device_id_type=MESH,
+        )
+
+    def shift(self, source, target, axis, step):
+        size = self.sizes[axis]
+        me = lax.axis_index(axis)
+        copy = self.copy(source, target, axis, lax.rem(me + step + size, size))
+        sends = (me + step >= 0) & (me + step < size)
+        gets = (me - step >= 0) & (me - step < size)
+        pl.when(sends)(copy.start)
+
+        def sent():
+            pl.when(sends)(copy.wait_send)
+
+        def got():
+            pl.when(gets)(copy.wait_recv)
+
+        return sent, got
+
+    def ahead(self, source, target, axis, sign):
+        me = lax.axis_index(axis)
+        return [
+            self.shift(source, target.at[me], axis, sign * step)
+            for step in range(1, self.sizes[axis])
+        ]
+
+    def everyone(self, source, target, axis, own, scatter=False):
+        size = self.sizes[axis]
+        me = lax.axis_index(axis)
+        waits = []
+        for step in range(1, size):
+            peer = lax.rem(me + step, size)
+            copy = self.copy(source.at[peer] if scatter else source, target.at[me], axis, peer)
+            copy.start()
+            waits.append((copy.wait_send, copy.wait_recv))
+        copy = pltpu.make_async_copy(source.at[me] if scatter else source, target.at[me], own)
+        copy.start()
+        waits.append((copy.wait,))
+        return waits
+
+
+def settle(waits):
+    for group in waits:
+        for wait in group:
+            wait()
+
+
+def link_call(kernel, name, cid, outs, args, copies, owns, scratch=()):
+    return pl.pallas_call(
+        kernel,
+        name=name,
+        out_shape=[jax.ShapeDtypeStruct(s, d) for s, d in outs],
+        in_specs=vmem(len(args)),
+        out_specs=vmem(len(outs)),
+        scratch_shapes=[
+            *scratch,
+            pltpu.SemaphoreType.DMA((copies,)),
+            pltpu.SemaphoreType.DMA((copies,)),
+            pltpu.SemaphoreType.DMA((owns,)),
+        ],
+        compiler_params=pltpu.CompilerParams(collective_id=cid, has_side_effects=True),
+    )(*args)
+
+
 def column(row):
     return jnp.broadcast_to(row, (LANES, LANES)).T
 
@@ -165,7 +253,8 @@
 
 
 def adjoint_kernel(
-    modes, g_ref, p_ref, w_ref, pass_ref, lead_ref, r_all_ref, r_ref, v_ref, q_out_ref, v3_ref
+    modes, g_ref, p_ref, w_ref, pass_ref, lead_ref, r_all_ref, r_ref, mid_ref, key_ref, gain_ref,
+    power_ref, v_ref, q_out_ref, sums_ref, v3_ref,
 ):
     rows, channels = v_ref.shape
     tiles = channels // LANES
@@ -194,8 +283,14 @@
 
         lax.fori_loop(0, rows - 1, back, tuple(start), unroll=2)
     inverse = 1.0 / column(r_row)
+    total = jnp.zeros((rows, LANES), F32)
     for j in range(tiles):
-        v_ref[:, j * LANES : (j + 1) * LANES] = v3_ref[pl.ds(j, rows, stride=tiles), :] * inverse
+        at = slice(j * LANES, (j + 1) * LANES)
+        v = v3_ref[pl.ds(j, rows, stride=tiles), :] * inverse
+        v_ref[:, at] = v
+        total = total + v * key_ref[:, at].astype(F32) * gain_ref[:, at] * mid_ref[:, at].astype(F32)
+    sums_ref[0] = power_ref[...]
+    sums_ref[1] = row8(total)
 
 
 def mix_kernel(width, x_ref, key_ref, gain_ref, pow_ref, mixed_ref):
@@ -207,21 +302,31 @@
 
 
 def conv_kernel(
-    members, x_ref, q_ref, mixed_ref, prev_ref, flip_ref, v_ref, key_ref, gain_ref,
-    conv_ref, mid_ref, sums_ref,
+    sizes, members, chunks, x_ref, q_ref, mixed_ref, flip_ref, lead_ref, share_ref,
+    conv_ref, mid_ref, power_ref, prev_ref, lead_all_ref, share_all_ref, send, recv, own,
 ):
     rows, channels = x_ref.shape
     fold = LANES // members
     row_ids = lax.broadcasted_iota(jnp.int32, (rows, LANES), 0)
     col_ids = lax.broadcasted_iota(jnp.int32, (rows, LANES), 1)
     owner = col_ids // members
-    fresh = lax.axis_index("ctx") > 0
-
-    def tile(j, sums):
+    link = Link(sizes, send, recv)
+    link.greet(["ctx"])
+    span = channels // chunks
+    pieces = [slice(c * span, (c + 1) * span) for c in range(chunks)]
+    halo = [
+        link.shift(mixed_ref.at[:, piece], prev_ref.at[:, piece], "ctx", 1) for piece in pieces
+    ]
+    waits = link.ahead(lead_ref, lead_all_ref, "ctx", -1)
+    waits += link.everyone(share_ref, share_all_ref, "ctx", own.at[0])
+
+    @pl.when(lax.axis_index("ctx") == 0)
+    def _():
+        prev_ref[...] = jnp.zeros_like(prev_ref)
+
+    def tile(j, power):
         at = lane_tile(j)
-        prev = prev_ref[:, at]
-        prev = jnp.where(fresh, prev, jnp.zeros_like(prev))
-        both = jnp.concatenate([prev, mixed_ref[:, at]], axis=0)
+        both = jnp.concatenate([prev_ref[:, at], mixed_ref[:, at]], axis=0)
         taps = flip_ref[pl.ds(pl.multiple_of(j * fold, fold), fold), :]
         conv = jnp.zeros((rows, LANES), F32)
         for g in range(fold):
@@ -238,13 +343,16 @@
         mid = (x_ref[:, at].astype(F32) + q_ref[:, at].astype(F32) * conv).astype(BF16)
         mid_ref[:, at] = mid
         mid = mid.astype(F32)
-        inner = v_ref[:, at] * key_ref[:, at].astype(F32) * gain_ref[:, at] * mid
-        return (sums[0] + mid * mid, sums[1] + inner)
-
-    zero = jnp.zeros((rows, LANES), F32)
-    power, inner = lax.fori_loop(0, channels // LANES, tile, (zero, zero))
-    sums_ref[0] = row8(power)
-    sums_ref[1] = row8(inner)
+        return power + mid * mid
+
+    power = jnp.zeros((rows, LANES), F32)
+    for c, (_, got) in enumerate(halo):
+        got()
+        power = lax.fori_loop(c * span // LANES, (c + 1) * span // LANES, tile, power)
+    power_ref[...] = row8(power)
+    for sent, _ in halo:
+        sent()
+    settle(waits)
 
 
 def middle_kernel(
@@ -269,7 +377,7 @@
         gkey_ref[:, at] = (v * normed).astype(BF16)
         u_ref[pl.ds(j, rows, stride=tiles), :] = key * normed * inverse
         grad = v * key
-        gain_part_ref[:, at] = jnp.sum(grad * mid * scale, axis=0, keepdims=True)
+        gain_part_ref[j : j + 1, :] = jnp.sum(grad * mid * scale, axis=0, keepdims=True)
         gmid = cot_ref[:, at].astype(F32) + gain * scale * grad - mid * pull
         gmid_ref[:, at] = gmid
         gq_ref[:, at] = (gmid * conv_ref[:, at]).astype(BF16)
@@ -297,11 +405,16 @@
 
 
 def state_kernel(
-    modes, u_ref, g_ref, p_ref, w_ref, pass_ref, fin_ref, r_all_ref, r_ref, q_ref, c_ref,
-    mid_ref, cot_ref, qli_ref, mixed_ref, gq_ref, res_ref, rate_ref, y_ref, in_ref,
+    sizes, modes, u_ref, g_ref, p_ref, w_ref, pass_ref, fin_ref, r_all_ref, r_ref, q_ref, c_ref,
+    mid_ref, cot_ref, qli_ref, inner_ref, small_ref, mixed_ref, gq_ref, grads_ref, inner_all_ref,
+    small_all_ref, y_ref, in_ref, send, recv, own,
 ):
     rows, channels = mid_ref.shape
     tiles = channels // LANES
+    link = Link(sizes, send, recv)
+    link.greet(["tp", "ctx"])
+    waits = link.everyone(inner_ref, inner_all_ref, "tp", own.at[0])
+    waits += link.everyone(small_ref, small_all_ref, "ctx", own.at[1], scatter=True)
     in_ref[...] = carried(fin_ref, r_all_ref, pass_ref, lax.axis_index("ctx"), False)
     sub = min(8, tiles)
     half = min(8, modes)
@@ -338,8 +451,10 @@
             for n in range(half):
                 at = where[n]
                 pgrad = weight[n] * psum[n] + q_ref[at, :] * slopes[n]
-                res_ref[at, :] = c_ref[0, at, :] * wsum[n]
-                rate_ref[at, :] = c_ref[1, at, :] * wsum[n] - c_ref[2, at, :] * pgrad
+                grads_ref[0, at, :] = (c_ref[0, at, :] * wsum[n]).astype(BF16)
+                grads_ref[1, at, :] = (
+                    c_ref[1, at, :] * wsum[n] - c_ref[2, at, :] * pgrad
+                ).astype(BF16)
     r_col = column(r_ref[:1, :])
     for j in range(tiles):
         at = slice(j * LANES, (j + 1) * LANES)
@@ -348,11 +463,13 @@
             mid_ref[:, at].astype(F32) + qli_ref[:, at].astype(F32) * conv
         ).astype(BF16)
         gq_ref[:, at] = (cot_ref[:, at].astype(F32) * conv).astype(BF16)
+    settle(waits)
 
 
 def back_kernel(
-    members, width, gconv_ref, next_ref, mixed_ref, prev_ref, filt_ref, x_ref, key_ref, gain_ref,
-    pow_ref, gkey_ref, gnorm_ref, gain_part_ref, inner_ref, fgrad_ref,
+    sizes, members, width, chunks, gconv_ref, mixed_ref, prev_ref, filt_ref, x_ref, key_ref,
+    gain_ref, pow_ref, fin_ref, gkey_ref, gnorm_ref, gain_part_ref, inner_ref, fgrad_ref,
+    fin_all_ref, next_ref, send, recv, own,
 ):
     rows, channels = x_ref.shape
     fold = LANES // members
@@ -360,19 +477,26 @@
     col_ids = lax.broadcasted_iota(jnp.int32, (rows, LANES), 1)
     owner = col_ids // members
     flip = jnp.where(row_ids + col_ids == rows - 1, 1.0, 0.0).astype(BF16)
-    place = lax.axis_index("ctx")
-    fresh = place > 0
-    more = place < lax.axis_size("ctx") - 1
+    link = Link(sizes, send, recv)
+    link.greet(["ctx"])
+    span = channels // chunks
+    pieces = [slice(c * span, (c + 1) * span) for c in range(chunks)]
+    halo = [
+        link.shift(gconv_ref.at[:, piece], next_ref.at[:, piece], "ctx", -1) for piece in pieces
+    ]
+    waits = link.ahead(fin_ref, fin_all_ref, "ctx", 1)
+
+    @pl.when(lax.axis_index("ctx") == sizes["ctx"] - 1)
+    def _():
+        next_ref[...] = jnp.zeros_like(next_ref)
+
     scale = column(lax.rsqrt(total_row(pow_ref) / width + EPSILON))
 
     def tile(j, inner):
         at = lane_tile(j)
         prev = prev_ref[:, at]
-        prev = jnp.where(fresh, prev, jnp.zeros_like(prev))
-        later = next_ref[:, at]
-        later = jnp.where(more, later, jnp.zeros_like(later))
-        own = gconv_ref[:, at]
-        both = jnp.concatenate([own, later], axis=0)
+        here = gconv_ref[:, at]
+        both = jnp.concatenate([here, next_ref[:, at]], axis=0)
         turned = jnp.concatenate(
             [
                 jnp.dot(flip, mixed_ref[:, at], preferred_element_type=F32).astype(BF16),
@@ -392,7 +516,7 @@
             high = jnp.where(col_ids < row_ids, table, 0.0).astype(BF16)
             out = jnp.dot(jnp.concatenate([low, high], axis=1), both, preferred_element_type=F32)
             gmix = jnp.where(owner == g, out, gmix)
-            mine = jnp.where(owner == g, own, jnp.zeros_like(own))
+            mine = jnp.where(owner == g, here, jnp.zeros_like(here))
             pair = lax.dot_general(
                 turned, mine, (((1,), (1,)), ((), ())), preferred_element_type=F32
             )
@@ -405,17 +529,26 @@
         gkey_ref[:, at] = (gmix * (x * gain * scale)).astype(BF16)
         gnorm = gmix * key_ref[:, at].astype(F32)
         gnorm_ref[:, at] = gnorm
-        gain_part_ref[:, at] = jnp.sum(gnorm * x * scale, axis=0, keepdims=True)
+        gain_part_ref[pl.ds(j, 1), :] = jnp.sum(gnorm * x * scale, axis=0, keepdims=True)
         return inner + gnorm * gain * x
 
-    inner = lax.fori_loop(0, channels // LANES, tile, jnp.zeros((rows, LANES), F32))
+    inner = jnp.zeros((rows, LANES), F32)
+    for c, (_, got) in enumerate(halo):
+        got()
+        inner = lax.fori_loop(c * span // LANES, (c + 1) * span // LANES, tile, inner)
     inner_ref[...] = row8(inner)
+    for sent, _ in halo:
+        sent()
+    settle(waits)
 
 
 def last_kernel(
-    width, factor, x_ref, gain_ref, gmid_ref, gnorm_ref, pow_ref, inner_ref, parts_ref,
-    out_ref, sum_ref,
+    sizes, width, factor, x_ref, gain_ref, gmid_ref, gnorm_ref, pow_ref, inner_ref, small_ref,
+    large_ref, out_ref, small_sum_ref, large_sum_ref, large_all_ref, send, recv, own,
 ):
+    link = Link(sizes, send, recv)
+    link.greet(["ctx"])
+    waits = link.everyone(large_ref, large_all_ref, "ctx", own.at[0], scatter=True)
     scale = column(lax.rsqrt(total_row(pow_ref) / width + EPSILON))
     pull = scale * scale * scale * column(total_row(inner_ref)) / width
     for j in range(x_ref.shape[1] // LANES):
@@ -425,10 +558,20 @@
             + gain_ref[:, at] * scale * gnorm_ref[:, at]
             - x_ref[:, at].astype(F32) * pull
         ).astype(BF16)
-    total = parts_ref[0].astype(F32)
-    for k in range(1, parts_ref.shape[0]):
-        total = total + parts_ref[k].astype(F32)
-    sum_ref[...] = (total * factor).astype(BF16)
+    settle(waits)
+    for parts_ref, sum_ref in ((small_ref, small_sum_ref), (large_all_ref, large_sum_ref)):
+        total = parts_ref[0].astype(F32)
+        for k in range(1, parts_ref.shape[0]):
+            total = total + parts_ref[k].astype(F32)
+        sum_ref[...] = (total * factor).astype(BF16)
+
+
+def pieces_of(parts, count):
+    height = parts.shape[0]
+    piece = -(-height // (16 * count)) * 16
+    if piece * count > height:
+        parts = jnp.pad(parts, ((0, piece * count - height), (0, 0)))
+    return parts.reshape(count, piece, LANES)
 
 
 def body(
@@ -481,76 +624,95 @@
         functools.partial(mix_kernel, width), "mix", [(full, BF16)],
         (tokens, key_mr, gain_mr, power_all),
     )
-    before = lax.ppermute(mixed_in, "ctx", [(k, k + 1) for k in range(ctx - 1)])
-    lead_all, shares_all = exchange(
-        [(lead, "ctx", False), (shares, "ctx", False)], sizes, 2, "gather_lead"
-    )
-    v, pulled = local_call(
+    chunks = min(4, tiles)
+    hops = chunks + ctx - 1
+    gathered = ((ctx,) + flat, BF16)
+    conv, middle, power_mid, before, lead_all, shares_all = link_call(
+        functools.partial(conv_kernel, sizes, members, chunks),
+        "conv",
+        2,
+        [
+            (full, F32), (full, BF16), ((8, rows), F32), (full, BF16), gathered,
+            ((ctx, 8, rows), F32),
+        ],
+        (tokens, query_mr, mixed_in, flipped, lead, shares),
+        hops + ctx - 1,
+        1,
+    )
+    v, pulled, sums = local_call(
         functools.partial(adjoint_kernel, modes),
         "adjoint",
-        [(full, F32), (flat, F32)],
-        (g_seq, poles, weight, passing, lead_all, shares_all, shares),
+        [(full, F32), (flat, F32), ((2, 8, rows), F32)],
+        (
+            g_seq, poles, weight, passing, lead_all, shares_all, shares, middle, key_li, gain_li,
+            power_mid,
+        ),
         [pltpu.VMEM((rows * tiles, LANES), F32)],
-    )
-    conv, middle, sums = local_call(
-        functools.partial(conv_kernel, members),
-        "conv",
-        [(full, F32), (full, BF16), ((2, 8, rows), F32)],
-        (tokens, query_mr, mixed_in, before, flipped, v, key_li, gain_li),
     )
     sums_all, = exchange([(sums, "tp", False)], sizes, 3, "gather_middle")
     grad_key_li, grad_mid, grad_query_mr, grad_conv, gain_li_part, u_seq = local_call(
         functools.partial(middle_kernel, width),
         "middle",
         [
-            (full, BF16), (full, F32), (full, BF16), (full, BF16), ((1, channels), F32),
+            (full, BF16), (full, F32), (full, BF16), (full, BF16), ((tiles, LANES), F32),
             ((rows * tiles, LANES), F32),
         ],
         (middle, key_li, gain_li, v, cotangent, query_mr, conv, shares, sums_all),
     )
-    after = lax.ppermute(grad_conv, "ctx", [(k + 1, k) for k in range(ctx - 1)])
     final, = local_call(
         functools.partial(finish_kernel, modes), "finish", [(flat, BF16)], (u_seq, poles, shares)
     )
-    final_all, = exchange([(final, "ctx", False)], sizes, 4, "gather_state")
-    mixed, grad_query_li, residue_part, rate_part = local_call(
-        functools.partial(state_kernel, modes),
+    gradient_key_medium, grad_norm, gain_mr_part, inner, filter_part, final_all, _ = link_call(
+        functools.partial(back_kernel, sizes, members, width, chunks),
+        "back",
+        4,
+        [
+            (full, BF16), (full, F32), ((tiles, LANES), F32), ((8, rows), F32),
+            ((groups, taps), F32), gathered, (full, BF16),
+        ],
+        (
+            grad_conv, mixed_in, before, wide, tokens, key_mr, gain_mr, power_all, final,
+        ),
+        hops,
+        1,
+    )
+    small = pieces_of(
+        jnp.concatenate([filter_part, gain_mr_part, gain_li_part], axis=0).astype(BF16), ctx
+    )
+    mixed, grad_query_li, mode_grads, inner_all, small_all = link_call(
+        functools.partial(state_kernel, sizes, modes),
         "state",
-        [(full, BF16), (full, BF16), (flat, F32), (flat, F32)],
+        5,
+        [
+            (full, BF16), (full, BF16), ((2,) + flat, BF16), ((tp, 8, rows), F32),
+            (small.shape, BF16),
+        ],
         (
             u_seq, g_seq, poles, weight, passing, final_all, shares_all, shares, pulled, consts,
-            middle, cotangent, query_li,
+            middle, cotangent, query_li, inner, small,
         ),
+        ctx + tp - 2,
+        2,
         [pltpu.VMEM((rows * tiles, LANES), F32), pltpu.VMEM(flat, F32)],
     )
-    gradient_key_medium, grad_norm, gain_mr_part, inner, filter_part = local_call(
-        functools.partial(back_kernel, members, width),
-        "back",
-        [(full, BF16), (full, F32), ((1, channels), F32), ((8, rows), F32), ((groups, taps), F32)],
-        (grad_conv, after, mixed_in, before, wide, tokens, key_mr, gain_mr, power_all),
-    )
-    parts = jnp.concatenate(
-        [
-            residue_part, rate_part, filter_part,
-            gain_mr_part.reshape(tiles, LANES), gain_li_part.reshape(tiles, LANES),
-        ],
-        axis=0,
-    ).astype(BF16)
-    height = parts.shape[0]
-    piece = -(-height // (16 * ctx)) * 16
-    parts = jnp.pad(parts, ((0, piece * ctx - height), (0, 0))).reshape(ctx, piece, LANES)
-    inner_all, parts_all = exchange(
-        [(inner, "tp", False), (parts, "ctx", True)], sizes, 5, "gather_last"
-    )
-    grad_tokens, sums_own = local_call(
-        functools.partial(last_kernel, width, factor),
+    size = modes * tiles
+    large = pieces_of(mode_grads.reshape(2 * size, LANES), ctx)
+    grad_tokens, small_sum, large_sum, _ = link_call(
+        functools.partial(last_kernel, sizes, width, factor),
         "last",
-        [(full, BF16), ((piece, LANES), BF16)],
-        (tokens, gain_mr, grad_mid, grad_norm, power_all, inner_all, parts_all),
-    )
-    totals, = exchange([(sums_own, "ctx", False)], sizes, 6, "gather_totals")
-    totals = totals.reshape(ctx * piece, LANES)[:height].astype(F32)
-    size = modes * tiles
+        6,
+        [(full, BF16), (small.shape[1:], BF16), (large.shape[1:], BF16), (large.shape, BF16)],
+        (
+            tokens, gain_mr, grad_mid, grad_norm, power_all, inner_all, small_all, large,
+        ),
+        ctx - 1,
+        1,
+    )
+    small_total, large_total = exchange(
+        [(small_sum, "ctx", False), (large_sum, "ctx", False)], sizes, 7, "gather_totals"
+    )
+    small_total = small_total.reshape(-1, LANES).astype(F32)
+    large_total = large_total.reshape(-1, LANES).astype(F32)
     return (
         mixed,
         grad_tokens,
@@ -558,11 +720,11 @@
         gradient_key_medium,
         grad_query_li,
         grad_key_li,
-        totals[2 * size + groups : 2 * size + groups + tiles].reshape(channels),
-        totals[2 * size + groups + tiles :].reshape(channels),
-        totals[2 * size : 2 * size + groups],
-        totals[:size].reshape(modes, channels),
-        totals[size : 2 * size].reshape(modes, channels),
+        small_total[groups : groups + tiles].reshape(channels),
+        small_total[groups + tiles : groups + 2 * tiles].reshape(channels),
+        small_total[:groups],
+        large_total[:size].reshape(modes, channels),
+        large_total[size : 2 * size].reshape(modes, channels),
     )
 
 

time: 156 us -> 137 us (0.88)
  Pallas kernels: 132 us -> 118 us
  starting transfers between devices: 5.4 us -> 0 us
  local copies, waits for them, and re-layouts: 8.74 us -> 12.4 us
  waiting for transfers between devices: 1.97 us -> 0 us
    pallas_call x0 -> x4, Pallas kernels: none -> 76.1 us  [link_call(): pl.pallas_call(kernel, name=name, out_shape=[jax.ShapeDtypeStruct(s, d) f...]
    pallas_call x6 -> x3, Pallas kernels: 74 us -> 19.7 us  [exchange(): pl.pallas_call(kernel, name=name, out_shape=outs, in_specs=vmem(count), o...]
    pallas_call x9 -> x5, Pallas kernels: 58.5 us -> 22.3 us  [local_call(): pl.pallas_call(kernel, name=name, out_shape=[jax.ShapeDtypeStruct(s, d) f...]
    ppermute x2 -> x0, starting transfers between devices: 5.4 us -> none  [the longest x1 4.11 us: body(): before = lax.ppermute(mixed_in, 'ctx', [(k, k + 1) for k in range(ctx - 1)])]
    unnamed x17 -> x24, local copies, waits for them, and re-layouts: 1.67 us -> 6.06 us
    ppermute x2 -> x0, waiting for transfers between devices: 1.97 us -> none  [the longest x1 1.97 us: body(): after = lax.ppermute(grad_conv, 'ctx', [(k + 1, k) for k in range(ctx - 1)])]
    unnamed x3 -> x0, other arithmetic: 1.81 us -> none
  transfers between devices with their start and end apart: 2 -> 0, of which waited for: 1 -> 0; matrix products, arithmetic and copies ran while one was open for 3% -> 0% of each run, Pallas kernels for 24% -> 0%
where the time goes in v2:
time: 137 us; the launch traced here: 136 us
  Pallas kernels  118 us (86%)
  local copies, waits for them, and re-layouts  12.4 us (9%)
  other arithmetic  4.83 us (4%)
    pallas_call x4, Pallas kernels, link_call(): pl.pallas_call(kernel, name=name, out_shape=[jax.ShapeDtypeStruct(s, d) f...  76.1 us
    pallas_call x5, Pallas kernels, local_call(): pl.pallas_call(kernel, name=name, out_shape=[jax.ShapeDtypeStruct(s, d) f...  22.3 us
    pallas_call x3, Pallas kernels, exchange(): pl.pallas_call(kernel, name=name, out_shape=outs, in_specs=vmem(count), o...  19.7 us
    unnamed x24, local copies, waits for them, and re-layouts  6.06 us

profile of v2, /device:TPU:0, one launch (start us, length us, event | category | flops | bytes accessed | tf_op | source)
XLA Modules:
  0.0 136.1 jit_solution(7771708589690353109)
XLA Ops:
  0.6 1.1 fusion.7
  1.7 0.7 exp.46.p_ref
  2.4 0.7 reshape.133.w_ref
  3.1 0.0 copy-done.9
  3.1 0.6 broadcast_in_dim.13.keep_ref
  3.7 4.6 %begin.1 = (f32[8,128]{1,0:T(8,128)}, f32[8,128]{1,0:T(8,128)}, f32[2048,128]{1,0:T(8,128)}, bf16[256,128]{1,0:T(8,128)(2,1)}) custom-call(bf16[128,2048]{1,0:T(8,128)(2,1)} %x_ref.9, bf16[128,2048]{1,0:T(8,128)(2,1)} %cot_ref.5, bf16[128,2048]{1,0:T(8,128)(2,1)} %qli_ref.1, f32[8,128]{1,0:T(8,128)} %broadcast_in_dim.13.keep_ref, f32[256,128]{1,0:T(8,128)} %exp.46.p_ref, ...), custom_call_target="tpu_custom_call" | custom-call | flops 10000000 | bytes 8000000 | tf_op jit(solution)/shard_map/begin/pallas_call | solution.py:23
  8.4 5.9 %gather_power.1.pow_ref = f32[4,8,128]{2,1,0:T(8,128)} custom-call(f32[8,128]{1,0:T(8,128)} %get-tuple-element.46.refs_0_), custom_call_target="tpu_custom_call" | custom-call | tf_op jit(solution)/shard_map/gather_power/pallas_call | solution.py:83
  14.3 0.0 copy-start
  14.3 2.3 %mix.1.mixed_ref = bf16[128,2048]{1,0:T(8,128)(2,1)} custom-call(bf16[128,2048]{1,0:T(8,128)(2,1)} %x_ref.9, bf16[128,2048]{1,0:T(8,128)(2,1)} %key_ref.7, f32[1,2048]{1,0:T(1,128)} %bitcast.13, f32[4,8,128]{2,1,0:T(8,128)} %gather_power.1.pow_ref), custom_call_target="tpu_custom_call" | custom-call | flops 10000000 | bytes 8000000 | tf_op jit(solution)/shard_map/mix/pallas_call | solution.py:23
  16.5 0.0 copy-done
  16.5 0.1 slice.35
  16.6 0.1 rev.3
  16.7 0.7 pad_maximum_fusion.1.flip_ref
  17.4 24.4 %conv.1 = (f32[128,2048]{1,0:T(8,128)}, bf16[128,2048]{1,0:T(8,128)(2,1)}, f32[8,128]{1,0:T(8,128)}, bf16[128,2048]{1,0:T(8,128)(2,1)}, bf16[8,256,128]{2,1,0:T(8,128)(2,1)}, /*index=5*/f32[8,8,128]{2,1,0:T(8,128)}) custom-call(bf16[128,2048]{1,0:T(8,128)(2,1)} %x_ref.9, bf16[128,2048]{1,0:T(8,128)(2,1)} %qmr_ref.1, bf16[128,2048]{1,0:T(8,128)(2,1)} %mix.1.mixed_ref, ...), custom_call_target="tpu_custom_call" | custom-call | tf_op jit(solution)/shard_map/conv/pallas_call | solution.py:170
  41.8 0.7 exp.48.pass_ref
  42.5 6.7 %adjoint.1 = (f32[128,2048]{1,0:T(8,128)}, f32[256,128]{1,0:T(8,128)}, f32[2,8,128]{2,1,0:T(8,128)}) custom-call(f32[2048,128]{1,0:T(8,128)} %get-tuple-element.50.g_ref, f32[256,128]{1,0:T(8,128)} %exp.46.p_ref, f32[256,128]{1,0:T(8,128)} %reshape.133.w_ref, f32[256,128]{1,0:T(8,128)} %exp.48.pass_ref, bf16[8,256,128]{2,1,0:T(8,128)(2,1)} %get-tuple-element.51.lead_ref, ...), custom_call_target="tpu_custom_call" | custom-call | flops 10000000 | bytes 8000000 | tf_op jit(solution)/shard_map/adjoint/pallas_call | solution.py:23
  49.2 5.0 %gather_middle.1.sums_ref = f32[4,2,8,128]{3,2,1,0:T(8,128)} custom-call(f32[2,8,128]{2,1,0:T(8,128)} %get-tuple-element.56.refs_0_), custom_call_target="tpu_custom_call" | custom-call | tf_op jit(solution)/shard_map/gather_middle/pallas_call | solution.py:83
  54.2 5.3 %middle.1 = (bf16[128,2048]{1,0:T(8,128)(2,1)}, f32[128,2048]{1,0:T(8,128)}, bf16[128,2048]{1,0:T(8,128)(2,1)}, bf16[128,2048]{1,0:T(8,128)(2,1)}, f32[16,128]{1,0:T(8,128)}, /*index=5*/f32[2048,128]{1,0:T(8,128)}) custom-call(bf16[128,2048]{1,0:T(8,128)(2,1)} %get-tuple-element.49.mid_ref, bf16[128,2048]{1,0:T(8,128)(2,1)} %key_ref.6, f32[1,2048]{1,0:T(1,128)} %bitcast.18, ...), custom_call_target="tpu_custom_call" | custom-call | flops 10000000 | bytes 8000000 | tf_op jit(solution)/shard_map/middle/pallas_call | solution.py:23
  59.5 3.3 %finish.1.fin_ref = bf16[256,128]{1,0:T(8,128)(2,1)} custom-call(f32[2048,128]{1,0:T(8,128)} %get-tuple-element.57.u_ref, f32[256,128]{1,0:T(8,128)} %exp.46.p_ref, f32[8,128]{1,0:T(8,128)} %get-tuple-element.48.share_ref.r_ref), custom_call_target="tpu_custom_call" | custom-call | flops 10000000 | bytes 8000000 | tf_op jit(solution)/shard_map/finish/pallas_call | solution.py:23
  62.9 0.6 convert_element_type.16.filt_ref
  63.5 23.1 %back.1 = (bf16[128,2048]{1,0:T(8,128)(2,1)}, f32[128,2048]{1,0:T(8,128)}, f32[16,128]{1,0:T(8,128)}, f32[8,128]{1,0:T(8,128)}, f32[128,128]{1,0:T(8,128)}, /*in...) custom-call(bf16[128,2048]{1,0:T(8,128)(2,1)} %get-tuple-element.58.gconv_ref, bf16[128,2048]{1,0:T(8,128)(2,1)} %mix.1.mixed_ref, ...), custom_call_target="tpu_custom_call" | custom-call | tf_op jit(solution)/shard_map/back/pallas_call | solution.py:170
  86.6 0.0 copy-start.8
  86.6 0.9 convert.9
  87.4 0.0 copy-done.8
  87.5 0.7 copy-done.7
  88.1 0.6 fusion.5
  88.8 0.9 copy-done.5
  89.7 0.1 fusion.3
  89.8 0.8 pad_maximum_fusion.c_ref
  90.6 19.3 %state.1 = (bf16[128,2048]{1,0:T(8,128)(2,1)}, bf16[128,2048]{1,0:T(8,128)(2,1)}, bf16[2,256,128]{2,1,0:T(8,128)(2,1)}, f32[4,8,128]{2,1,0:T(8,128)}, bf16[8,32,128]{2,1,0:T(8,128)(2,1)}) custom-call(f32[2048,128]{1,0:T(8,128)} %get-tuple-element.57.u_ref, f32[2048,128]{1,0:T(8,128)} %get-tuple-element.50.g_ref, f32[256,128]{1,0:T(8,128)} %exp.46.p_ref, ...), custom_call_target="tpu_custom_call" | custom-call | tf_op jit(solution)/shard_map/state/pallas_call | solution.py:170
  109.9 9.3 %last.1 = (bf16[128,2048]{1,0:T(8,128)(2,1)}, bf16[32,128]{1,0:T(8,128)(2,1)}, bf16[64,128]{1,0:T(8,128)(2,1)}, bf16[8,64,128]{2,1,0:T(8,128)(2,1)}) custom-call(bf16[128,2048]{1,0:T(8,128)(2,1)} %x_ref.9, f32[1,2048]{1,0:T(1,128)} %bitcast.15, f32[128,2048]{1,0:T(8,128)} %get-tuple-element.67.gmid_ref, f32[128,2048]{1,0:T(8,128)} %get-tuple-element.68.gnorm_ref, ...), custom_call_target="tpu_custom_call" | custom-call | tf_op jit(solution)/shard_map/last/pallas_call | solution.py:170
  119.2 8.8 %gather_totals.1 = (bf16[8,32,128]{2,1,0:T(8,128)(2,1)}, bf16[8,64,128]{2,1,0:T(8,128)(2,1)}) custom-call(bf16[32,128]{1,0:T(8,128)(2,1)} %get-tuple-element.77.refs_0_, bf16[64,128]{1,0:T(8,128)(2,1)} %get-tuple-element.78.refs_1_), custom_call_target="tpu_custom_call" | custom-call | tf_op jit(solution)/shard_map/gather_totals/pallas_call | solution.py:83
  128.1 0.0 copy-start.6
  128.1 0.9 fusion.6
  129.0 0.0 copy-start.3
  129.0 0.7 reshape.130
  129.7 0.7 reshape.131
  130.4 0.0 copy-done.6
  130.4 0.6 slice_bitcast_fusion
  131.0 0.6 slice.38
  131.6 0.0 copy-done.3
  131.6 0.8 copy.27
  132.4 0.4 copy-done.4
  132.9 0.8 copy.28
  133.7 0.4 copy-done.1
  134.1 0.8 copy.29
  134.9 0.4 copy-done.2
  135.3 0.8 copy.30
  (12 shorter events, 0.1 us)
Async XLA Ops:
  2.4 0.7 copy-start.9
  14.3 2.3 %copy-start = (bf16[128,128]{1,0:T(8,128)(2,1)S(1)}, bf16[128,128]{1,0:T(8,128)(2,1)}, u32[]{:S(2)}) copy-start(bf16[128,128]{1,0:T(8,128)(2,1)} %param.16) | copy-start | bytes 98308
  86.6 0.9 copy-start.8
  87.4 0.7 copy-start.7
  88.8 0.9 copy-start.5
  128.1 2.3 %copy-start.6 = (bf16[8,32,128]{2,1,0:T(8,128)(2,1)S(1)}, bf16[8,32,128]{2,1,0:T(8,128)(2,1)}, u32[]{:S(2)}) copy-start(bf16[8,32,128]{2,1,0:T(8,128)(2,1)} %get-tuple-element.79) | copy-start | bytes 196612
  129.0 2.6 %copy-start.3 = (bf16[128,2048]{1,0:T(8,128)(2,1)S(1)}, bf16[128,2048]{1,0:T(8,128)(2,1)}, u32[]{:S(2)}) copy-start(bf16[128,2048]{1,0:T(8,128)(2,1)} %get-tuple-element.103) | copy-start | bytes 1572868
  131.6 1.2 copy-start.4
  132.9 1.2 copy-start.1
  134.1 1.2 copy-start.2

commit v3 on v2

--- a/solution.py
+++ b/solution.py
@@ -138,13 +138,6 @@
 
         return sent, got
 
-    def ahead(self, source, target, axis, sign):
-        me = lax.axis_index(axis)
-        return [
-            self.shift(source, target.at[me], axis, sign * step)
-            for step in range(1, self.sizes[axis])
-        ]
-
     def everyone(self, source, target, axis, own, scatter=False):
         size = self.sizes[axis]
         me = lax.axis_index(axis)
@@ -240,27 +233,61 @@
             lead_ref[where[n], :] = (w_ref[where[n], :] * pole[n] * units[n]).astype(BF16)
 
 
-def carried(part_ref, r_all_ref, pass_ref, ahead, reverse):
-    count = part_ref.shape[0]
-    order = range(count - 1, 0, -1) if reverse else range(count - 1)
-    acc = jnp.zeros(pass_ref.shape, F32)
-    for m in order:
-        share = jnp.broadcast_to(r_all_ref[m][:1, LANES - 1 :], (1, LANES))
-        new = part_ref[m].astype(F32) + pass_ref[...] * share * acc
-        live = m > ahead if reverse else m < ahead
-        acc = jnp.where(live, new, acc)
-    return acc
+def doubling(link, own_ref, got_ref, part_ref, share_all_ref, pass_ref, out_ref, sign, ready):
+    size = link.sizes["ctx"]
+    me = lax.axis_index("ctx")
+    rounds = got_ref.shape[0]
+    sends = [None] * rounds
+    sends[0] = link.shift(own_ref, got_ref.at[0], "ctx", sign)
+
+    def share(index):
+        row = share_all_ref[lax.rem(index + size, size)][:1, LANES - 1 :]
+        return jnp.broadcast_to(row, (1, LANES))
+
+    def receive(k):
+        if k == 0:
+            ready()
+        sends[k][1]()
+        reach = 2**k
+        source = me - sign * reach
+        live = (source >= 0) & (source < size)
+        value = jnp.where(live, got_ref[k].astype(F32), 0.0)
+        if k > 0:
+            factor = pass_ref[...]
+            for step in range(1, k):
+                factor = factor * factor * pass_ref[...]
+            scale = share(me - sign)
+            for step in range(2, reach):
+                scale = scale * share(me - sign * step)
+            value = out_ref[...] + factor * scale * value
+        out_ref[...] = value
+        if k < rounds - 1:
+            joined = own_ref[...].astype(F32) + pass_ref[...] * share(me) * value
+            part_ref[k] = joined.astype(BF16)
+
+    def send(k):
+        sends[k] = link.shift(part_ref.at[k - 1], got_ref.at[k], "ctx", sign * 2**k)
+
+    stages = [functools.partial(receive, 0)]
+    for k in range(1, rounds):
+        stages += [functools.partial(send, k), functools.partial(receive, k)]
+
+    def done():
+        for sent, _ in sends:
+            sent()
+
+    return stages, done
 
 
 def adjoint_kernel(
-    modes, g_ref, p_ref, w_ref, pass_ref, lead_ref, r_all_ref, r_ref, mid_ref, key_ref, gain_ref,
+    modes, g_ref, p_ref, w_ref, lead_ref, r_ref, mid_ref, key_ref, gain_ref,
     power_ref, v_ref, q_out_ref, sums_ref, v3_ref,
 ):
     rows, channels = v_ref.shape
     tiles = channels // LANES
     r_row = r_ref[:1, :]
     r_end = jnp.broadcast_to(r_row[:, LANES - 1 :], (1, LANES))
-    q_out_ref[...] = carried(lead_ref, r_all_ref, pass_ref, lax.axis_index("ctx"), True) * r_end
+    q_out_ref[...] = lead_ref[...] * r_end
     sub = min(8, tiles)
     for b in range(tiles // sub):
         where = [pl.ds(n * tiles + b * sub, sub) for n in range(modes)]
@@ -302,8 +329,9 @@
 
 
 def conv_kernel(
-    sizes, members, chunks, x_ref, q_ref, mixed_ref, flip_ref, lead_ref, share_ref,
-    conv_ref, mid_ref, power_ref, prev_ref, lead_all_ref, share_all_ref, send, recv, own,
+    sizes, members, chunks, x_ref, q_ref, mixed_ref, flip_ref, lead_ref, share_ref, pass_ref,
+    conv_ref, mid_ref, power_ref, prev_ref, lead_all_ref, share_all_ref, got_ref, part_ref,
+    send, recv, own,
 ):
     rows, channels = x_ref.shape
     fold = LANES // members
@@ -314,11 +342,14 @@
     link.greet(["ctx"])
     span = channels // chunks
     pieces = [slice(c * span, (c + 1) * span) for c in range(chunks)]
+    waits = link.everyone(share_ref, share_all_ref, "ctx", own.at[0])
+    stages, done = doubling(
+        link, lead_ref, got_ref, part_ref, share_all_ref, pass_ref, lead_all_ref, -1,
+        lambda: settle(waits),
+    )
     halo = [
         link.shift(mixed_ref.at[:, piece], prev_ref.at[:, piece], "ctx", 1) for piece in pieces
     ]
-    waits = link.ahead(lead_ref, lead_all_ref, "ctx", -1)
-    waits += link.everyone(share_ref, share_all_ref, "ctx", own.at[0])
 
     @pl.when(lax.axis_index("ctx") == 0)
     def _():
@@ -347,12 +378,16 @@
 
     power = jnp.zeros((rows, LANES), F32)
     for c, (_, got) in enumerate(halo):
+        if c < len(stages):
+            stages[c]()
         got()
         power = lax.fori_loop(c * span // LANES, (c + 1) * span // LANES, tile, power)
     power_ref[...] = row8(power)
+    for stage in stages[chunks:]:
+        stage()
     for sent, _ in halo:
         sent()
-    settle(waits)
+    done()
 
 
 def middle_kernel(
@@ -405,9 +440,9 @@
 
 
 def state_kernel(
-    sizes, modes, u_ref, g_ref, p_ref, w_ref, pass_ref, fin_ref, r_all_ref, r_ref, q_ref, c_ref,
+    sizes, modes, u_ref, g_ref, p_ref, w_ref, in_ref, r_ref, q_ref, c_ref,
     mid_ref, cot_ref, qli_ref, inner_ref, small_ref, mixed_ref, gq_ref, grads_ref, inner_all_ref,
-    small_all_ref, y_ref, in_ref, send, recv, own,
+    small_all_ref, y_ref, send, recv, own,
 ):
     rows, channels = mid_ref.shape
     tiles = channels // LANES
@@ -415,7 +450,6 @@
     link.greet(["tp", "ctx"])
     waits = link.everyone(inner_ref, inner_all_ref, "tp", own.at[0])
     waits += link.everyone(small_ref, small_all_ref, "ctx", own.at[1], scatter=True)
-    in_ref[...] = carried(fin_ref, r_all_ref, pass_ref, lax.axis_index("ctx"), False)
     sub = min(8, tiles)
     half = min(8, modes)
     zero = jnp.zeros((sub, LANES), F32)
@@ -468,8 +502,8 @@
 
 def back_kernel(
     sizes, members, width, chunks, gconv_ref, mixed_ref, prev_ref, filt_ref, x_ref, key_ref,
-    gain_ref, pow_ref, fin_ref, gkey_ref, gnorm_ref, gain_part_ref, inner_ref, fgrad_ref,
-    fin_all_ref, next_ref, send, recv, own,
+    gain_ref, pow_ref, fin_ref, share_all_ref, pass_ref, gkey_ref, gnorm_ref, gain_part_ref, inner_ref, fgrad_ref,
+    fin_all_ref, next_ref, got_ref, part_ref, send, recv, own,
 ):
     rows, channels = x_ref.shape
     fold = LANES // members
@@ -481,10 +515,12 @@
     link.greet(["ctx"])
     span = channels // chunks
     pieces = [slice(c * span, (c + 1) * span) for c in range(chunks)]
+    stages, done = doubling(
+        link, fin_ref, got_ref, part_ref, share_all_ref, pass_ref, fin_all_ref, 1, lambda: None
+    )
     halo = [
         link.shift(gconv_ref.at[:, piece], next_ref.at[:, piece], "ctx", -1) for piece in pieces
     ]
-    waits = link.ahead(fin_ref, fin_all_ref, "ctx", 1)
 
     @pl.when(lax.axis_index("ctx") == sizes["ctx"] - 1)
     def _():
@@ -534,12 +570,16 @@
 
     inner = jnp.zeros((rows, LANES), F32)
     for c, (_, got) in enumerate(halo):
+        if c < len(stages):
+            stages[c]()
         got()
         inner = lax.fori_loop(c * span // LANES, (c + 1) * span // LANES, tile, inner)
     inner_ref[...] = row8(inner)
+    for stage in stages[chunks:]:
+        stage()
     for sent, _ in halo:
         sent()
-    settle(waits)
+    done()
 
 
 def last_kernel(
@@ -625,8 +665,12 @@
         (tokens, key_mr, gain_mr, power_all),
     )
     chunks = min(4, tiles)
-    hops = chunks + ctx - 1
-    gathered = ((ctx,) + flat, BF16)
+    rounds = max(1, (ctx - 1).bit_length())
+    hops = chunks + rounds
+    gathered = (flat, F32)
+    slots = [
+        pltpu.VMEM((rounds,) + flat, BF16), pltpu.VMEM((max(1, rounds - 1),) + flat, BF16),
+    ]
     conv, middle, power_mid, before, lead_all, shares_all = link_call(
         functools.partial(conv_kernel, sizes, members, chunks),
         "conv",
@@ -635,16 +679,17 @@
             (full, F32), (full, BF16), ((8, rows), F32), (full, BF16), gathered,
             ((ctx, 8, rows), F32),
         ],
-        (tokens, query_mr, mixed_in, flipped, lead, shares),
+        (tokens, query_mr, mixed_in, flipped, lead, shares, passing),
         hops + ctx - 1,
         1,
+        slots,
     )
     v, pulled, sums = local_call(
         functools.partial(adjoint_kernel, modes),
         "adjoint",
         [(full, F32), (flat, F32), ((2, 8, rows), F32)],
         (
-            g_seq, poles, weight, passing, lead_all, shares_all, shares, middle, key_li, gain_li,
+            g_seq, poles, weight, lead_all, shares, middle, key_li, gain_li,
             power_mid,
         ),
         [pltpu.VMEM((rows * tiles, LANES), F32)],
@@ -672,9 +717,11 @@
         ],
         (
             grad_conv, mixed_in, before, wide, tokens, key_mr, gain_mr, power_all, final,
+            shares_all, passing,
         ),
         hops,
         1,
+        slots,
     )
     small = pieces_of(
         jnp.concatenate([filter_part, gain_mr_part, gain_li_part], axis=0).astype(BF16), ctx
@@ -688,12 +735,12 @@
             (small.shape, BF16),
         ],
         (
-            u_seq, g_seq, poles, weight, passing, final_all, shares_all, shares, pulled, consts,
+            u_seq, g_seq, poles, weight, final_all, shares, pulled, consts,
             middle, cotangent, query_li, inner, small,
         ),
         ctx + tp - 2,
         2,
-        [pltpu.VMEM((rows * tiles, LANES), F32), pltpu.VMEM(flat, F32)],
+        [pltpu.VMEM((rows * tiles, LANES), F32)],
     )
     size = modes * tiles
     large = pieces_of(mode_grads.reshape(2 * size, LANES), ctx)

time: 137 us -> 146 us (1.066)
  Pallas kernels: 118 us -> 127 us
    pallas_call x4, Pallas kernels: 76.1 us -> 85.4 us  [link_call(): pl.pallas_call(kernel, name=name, out_shape=[jax.ShapeDtypeStruct(s, d) f...]
where the time goes in v3:
time: 146 us; the launch traced here: 145 us
  Pallas kernels  127 us (87%)
  local copies, waits for them, and re-layouts  12.5 us (9%)
  other arithmetic  4.83 us (3%)
    pallas_call x4, Pallas kernels, link_call(): pl.pallas_call(kernel, name=name, out_shape=[jax.ShapeDtypeStruct(s, d) f...  85.4 us
    pallas_call x5, Pallas kernels, local_call(): pl.pallas_call(kernel, name=name, out_shape=[jax.ShapeDtypeStruct(s, d) f...  21.9 us
    pallas_call x3, Pallas kernels, exchange(): pl.pallas_call(kernel, name=name, out_shape=outs, in_specs=vmem(count), o...  19.6 us
    unnamed x24, local copies, waits for them, and re-layouts  6.13 us

profile of v3, /device:TPU:0, one launch (start us, length us, event | category | flops | bytes accessed | tf_op | source)
XLA Modules:
  0.0 145.0 jit_solution(240712144630743058)
XLA Ops:
  0.6 1.1 fusion.7
  1.7 0.7 exp.46.p_ref
  2.4 0.0 copy-start.9
  2.4 0.7 reshape.133.w_ref
  3.1 0.0 copy-done.9
  3.1 0.6 broadcast_in_dim.13.keep_ref
  3.7 4.6 %begin.1 = (f32[8,128]{1,0:T(8,128)}, f32[8,128]{1,0:T(8,128)}, f32[2048,128]{1,0:T(8,128)}, bf16[256,128]{1,0:T(8,128)(2,1)}) custom-call(bf16[128,2048]{1,0:T(8,128)(2,1)} %x_ref.9, bf16[128,2048]{1,0:T(8,128)(2,1)} %cot_ref.5, bf16[128,2048]{1,0:T(8,128)(2,1)} %qli_ref.1, f32[8,128]{1,0:T(8,128)} %broadcast_in_dim.13.keep_ref, f32[256,128]{1,0:T(8,128)} %exp.46.p_ref, ...), custom_call_target="tpu_custom_call" | custom-call | flops 10000000 | bytes 8000000 | tf_op jit(solution)/shard_map/begin/pallas_call | solution.py:23
  8.4 5.9 %gather_power.1.pow_ref = f32[4,8,128]{2,1,0:T(8,128)} custom-call(f32[8,128]{1,0:T(8,128)} %get-tuple-element.46.refs_0_), custom_call_target="tpu_custom_call" | custom-call | tf_op jit(solution)/shard_map/gather_power/pallas_call | solution.py:83
  14.3 2.3 %mix.1.mixed_ref = bf16[128,2048]{1,0:T(8,128)(2,1)} custom-call(bf16[128,2048]{1,0:T(8,128)(2,1)} %x_ref.9, bf16[128,2048]{1,0:T(8,128)(2,1)} %key_ref.7, f32[1,2048]{1,0:T(1,128)} %bitcast.13, f32[4,8,128]{2,1,0:T(8,128)} %gather_power.1.pow_ref), custom_call_target="tpu_custom_call" | custom-call | flops 10000000 | bytes 8000000 | tf_op jit(solution)/shard_map/mix/pallas_call | solution.py:23
  16.5 0.7 exp.48.pass_ref
  17.2 0.1 copy-done
  17.3 0.1 slice.35
  17.4 0.1 rev.3
  17.5 0.7 pad_maximum_fusion.1.flip_ref
  18.2 31.2 %conv.1 = (f32[128,2048]{1,0:T(8,128)}, bf16[128,2048]{1,0:T(8,128)(2,1)}, f32[8,128]{1,0:T(8,128)}, bf16[128,2048]{1,0:T(8,128)(2,1)}, f32[256,128]{1,0:T(8,128)}, /*index=5*/f32[8,8,128]{2,1,0:T(8,128)}) custom-call(bf16[128,2048]{1,0:T(8,128)(2,1)} %x_ref.9, bf16[128,2048]{1,0:T(8,128)(2,1)} %qmr_ref.1, bf16[128,2048]{1,0:T(8,128)(2,1)} %mix.1.mixed_ref, ...), custom_call_target="tpu_custom_call" | custom-call | tf_op jit(solution)/shard_map/conv/pallas_call | solution.py:163
  49.4 6.3 %adjoint.1 = (f32[128,2048]{1,0:T(8,128)}, f32[256,128]{1,0:T(8,128)}, f32[2,8,128]{2,1,0:T(8,128)}) custom-call(f32[2048,128]{1,0:T(8,128)} %get-tuple-element.50.g_ref, f32[256,128]{1,0:T(8,128)} %exp.46.p_ref, f32[256,128]{1,0:T(8,128)} %reshape.133.w_ref, f32[256,128]{1,0:T(8,128)} %get-tuple-element.51.lead_ref, ...), custom_call_target="tpu_custom_call" | custom-call | flops 10000000 | bytes 8000000 | tf_op jit(solution)/shard_map/adjoint/pallas_call | solution.py:23
  55.7 5.0 %gather_middle.1.sums_ref = f32[4,2,8,128]{3,2,1,0:T(8,128)} custom-call(f32[2,8,128]{2,1,0:T(8,128)} %get-tuple-element.55.refs_0_), custom_call_target="tpu_custom_call" | custom-call | tf_op jit(solution)/shard_map/gather_middle/pallas_call | solution.py:83
  60.8 5.3 %middle.1 = (bf16[128,2048]{1,0:T(8,128)(2,1)}, f32[128,2048]{1,0:T(8,128)}, bf16[128,2048]{1,0:T(8,128)(2,1)}, bf16[128,2048]{1,0:T(8,128)(2,1)}, f32[16,128]{1,0:T(8,128)}, /*index=5*/f32[2048,128]{1,0:T(8,128)}) custom-call(bf16[128,2048]{1,0:T(8,128)(2,1)} %get-tuple-element.49.mid_ref, bf16[128,2048]{1,0:T(8,128)(2,1)} %key_ref.6, f32[1,2048]{1,0:T(1,128)} %bitcast.18, ...), custom_call_target="tpu_custom_call" | custom-call | flops 10000000 | bytes 8000000 | tf_op jit(solution)/shard_map/middle/pallas_call | solution.py:23
  66.1 3.3 %finish.1.fin_ref = bf16[256,128]{1,0:T(8,128)(2,1)} custom-call(f32[2048,128]{1,0:T(8,128)} %get-tuple-element.56.u_ref, f32[256,128]{1,0:T(8,128)} %exp.46.p_ref, f32[8,128]{1,0:T(8,128)} %get-tuple-element.48.share_ref.r_ref), custom_call_target="tpu_custom_call" | custom-call | flops 10000000 | bytes 8000000 | tf_op jit(solution)/shard_map/finish/pallas_call | solution.py:23
  69.4 0.6 convert_element_type.16.filt_ref
  70.1 20.5 %back.1 = (bf16[128,2048]{1,0:T(8,128)(2,1)}, f32[128,2048]{1,0:T(8,128)}, f32[16,128]{1,0:T(8,128)}, f32[8,128]{1,0:T(8,128)}, f32[128,128]{1,0:T(8,128)}, /*in...) custom-call(bf16[128,2048]{1,0:T(8,128)(2,1)} %get-tuple-element.57.gconv_ref, bf16[128,2048]{1,0:T(8,128)(2,1)} %mix.1.mixed_ref, ...), custom_call_target="tpu_custom_call" | custom-call | tf_op jit(solution)/shard_map/back/pallas_call | solution.py:163
  90.6 0.0 copy-start.8
  90.6 0.9 convert.9
  91.5 0.0 copy-done.8
  91.5 0.7 copy-done.7
  92.2 0.6 fusion.5
  92.8 0.9 copy-done.5
  93.7 0.1 fusion.3
  93.9 0.8 pad_maximum_fusion.c_ref
  94.6 24.3 %state.1 = (bf16[128,2048]{1,0:T(8,128)(2,1)}, bf16[128,2048]{1,0:T(8,128)(2,1)}, bf16[2,256,128]{2,1,0:T(8,128)(2,1)}, f32[4,8,128]{2,1,0:T(8,128)}, bf16[8,32,128]{2,1,0:T(8,128)(2,1)}) custom-call(f32[2048,128]{1,0:T(8,128)} %get-tuple-element.56.u_ref, f32[2048,128]{1,0:T(8,128)} %get-tuple-element.50.g_ref, f32[256,128]{1,0:T(8,128)} %exp.46.p_ref, ...), custom_call_target="tpu_custom_call" | custom-call | tf_op jit(solution)/shard_map/state/pallas_call | solution.py:163
  119.0 9.3 %last.1 = (bf16[128,2048]{1,0:T(8,128)(2,1)}, bf16[32,128]{1,0:T(8,128)(2,1)}, bf16[64,128]{1,0:T(8,128)(2,1)}, bf16[8,64,128]{2,1,0:T(8,128)(2,1)}) custom-call(bf16[128,2048]{1,0:T(8,128)(2,1)} %x_ref.9, f32[1,2048]{1,0:T(1,128)} %bitcast.15, f32[128,2048]{1,0:T(8,128)} %get-tuple-element.67.gmid_ref, f32[128,2048]{1,0:T(8,128)} %get-tuple-element.68.gnorm_ref, ...), custom_call_target="tpu_custom_call" | custom-call | tf_op jit(solution)/shard_map/last/pallas_call | solution.py:163
  128.2 8.7 %gather_totals.1 = (bf16[8,32,128]{2,1,0:T(8,128)(2,1)}, bf16[8,64,128]{2,1,0:T(8,128)(2,1)}) custom-call(bf16[32,128]{1,0:T(8,128)(2,1)} %get-tuple-element.77.refs_0_, bf16[64,128]{1,0:T(8,128)(2,1)} %get-tuple-element.78.refs_1_), custom_call_target="tpu_custom_call" | custom-call | tf_op jit(solution)/shard_map/gather_totals/pallas_call | solution.py:83
  136.9 0.0 copy-start.6
  136.9 0.9 fusion.6
  137.8 0.0 copy-start.3
  137.8 0.7 reshape.130
  138.5 0.7 reshape.131
  139.2 0.0 copy-done.6
  139.2 0.6 slice_bitcast_fusion
  139.8 0.6 slice.38
  140.5 0.0 copy-done.3
  140.5 0.8 copy.27
  141.3 0.4 copy-done.4
  141.7 0.8 copy.28
  142.5 0.4 copy-done.1
  142.9 0.8 copy.29
  143.7 0.4 copy-done.2
  144.2 0.8 copy.30
  (12 shorter events, 0.1 us)
Async XLA Ops:
  2.4 0.7 copy-start.9
  16.5 0.8 copy-start
  90.6 0.9 copy-start.8
  91.5 0.7 copy-start.7
  92.8 0.9 copy-start.5
  136.9 2.3 %copy-start.6 = (bf16[8,32,128]{2,1,0:T(8,128)(2,1)S(1)}, bf16[8,32,128]{2,1,0:T(8,128)(2,1)}, u32[]{:S(2)}) copy-start(bf16[8,32,128]{2,1,0:T(8,128)(2,1)} %get-tuple-element.79) | copy-start | bytes 196612
  137.8 2.6 %copy-start.3 = (bf16[128,2048]{1,0:T(8,128)(2,1)S(1)}, bf16[128,2048]{1,0:T(8,128)(2,1)}, u32[]{:S(2)}) copy-start(bf16[128,2048]{1,0:T(8,128)(2,1)} %get-tuple-element.103) | copy-start | bytes 1572868
  140.5 1.2 copy-start.4
  141.7 1.2 copy-start.1
  142.9 1.2 copy-start.2
